TPU v7x, 512 devices: a whole 4x4x16 slice. The times are simulated.
512 devices in a mesh: lat: 32 (over z, core), lev: 16 (over x, y).
Axes of the slice: x: 4, y: 4, z: 16, core: 2. Of those that a mesh axis runs over, the one named last changes fastest.
Arguments:
- zonal_wind: float32 [64, 256, 2880], P('lev', 'lat'), may hold values from -1 to 1
- merid_wind: float32 [64, 256, 2880], P('lev', 'lat'), may hold values from -1 to 1
- thickness: float32 [64, 256, 2880], P('lev', 'lat'), may hold values from 0.6 to 1.8
- potential_temp: float32 [64, 256, 2880], P('lev', 'lat'), may hold values from 0.5 to 2
- cutoff: int32 [32], replicated, may hold values from 4 to 255, as said below
- sigma_weights: float32 [64], replicated, may hold values from 0.5 to 2
Outputs:
- remapped_wind: float32 [64, 256, 2880], P(None, 'lat', 'lev')
- remapped_temp: float32 [64, 256, 2880], P(None, 'lat', 'lev')
Inputs may be any that keep to these rules, and one draw needn't show every extreme that they name: `cutoff`: cutoff wavenumber of each filtered row, southern rows in row order, then northern rows in row order.
All inputs are finite; a program needn't handle non-finite values.
Results may differ from a plain program's by a relative error of at most 0.0003.
Values sent between devices are 32-bit elements; how exact they have to be, the bound alone decides.
No kernel may reach another device: no remote copies, remote signals or barrier semaphores. Data moves between devices by JAX's collectives and lax.ppermute only.
A program may use at most 64 MiB of HBM per device.

v0:
```python
import math

import jax
import jax.numpy as jnp
from jax import lax
from jax.sharding import PartitionSpec as P

POLAR_BANDS = 2
KMAX = 256


COURANT = 0.02
PRESSURE_COEF = 0.05
HIGHEST = lax.Precision.HIGHEST


def with_halo(x, sides, width):
    for axis, dim in sides:
        count, length = (lax.axis_size(axis), x.shape[dim])
        up = [(i, (i + 1) % count) for i in range(count - 1)]
        down = [(j, i) for i, j in up]
        last = lax.slice_in_dim(x, length - width, length, axis=dim)
        first = lax.slice_in_dim(x, 0, width, axis=dim)
        before = lax.ppermute(last, axis, up)
        after = lax.ppermute(first, axis, down)
        x = jnp.concatenate([before, x, after], axis=dim)
    return x


def prefix(part, axis, combine, identity):
    place = lax.axis_index(axis)
    gathered = lax.all_gather(part, axis)
    state = jnp.zeros_like(part) + jnp.asarray(identity, part.dtype)

    def one(lap, state):
        return combine(state, lax.dynamic_index_in_dim(gathered, lap, 0, False))

    return lax.fori_loop(0, place, one, state)


def flux_zonal(quantity, wind):
    face_wind = 0.5 * (wind + jnp.roll(wind, 1, axis=-1))
    face_flux = face_wind * 0.5 * (quantity + jnp.roll(quantity, 1, axis=-1))
    return jnp.roll(face_flux, -1, axis=-1) - face_flux


def flux_merid(padded_field, padded_wind):
    face_flux = (
        0.25
        * (padded_wind[:, :-1] + padded_wind[:, 1:])
        * (padded_field[:, :-1] + padded_field[:, 1:])
    )
    return face_flux[:, 1:] - face_flux[:, :-1]


def advance(thickness, potential, zonal, merid_pad, thick_pad, temp_pad):
    heat = thickness * potential
    heat_pad = thick_pad * temp_pad
    new_thick = thickness - COURANT * (
        flux_zonal(thickness, zonal) + flux_merid(thick_pad, merid_pad)
    )
    new_heat = heat - COURANT * (flux_zonal(heat, zonal) + flux_merid(heat_pad, merid_pad))
    return (new_thick, new_heat / new_thick)


def pressure_push(zonal, mid_pressure):
    return zonal - PRESSURE_COEF * (
        jnp.roll(mid_pressure, -1, axis=-1) - jnp.roll(mid_pressure, 1, axis=-1)
    )


def ppm_edges(fields):
    halves = 0.5 * (fields[:, :-1] + fields[:, 1:])
    fourth = 7.0 / 12.0 * (fields[:, 1:-2] + fields[:, 2:-1]) - 1.0 / 12.0 * (
        fields[:, :-3] + fields[:, 3:]
    )
    return jnp.concatenate(
        [fields[:, :1], halves[:, :1], fourth, halves[:, -1:], fields[:, -1:]], axis=1
    )


def remap_columns(fields, thickness, weights):
    levels = thickness.shape[0]
    field_count = fields.shape[0]
    flat_thick = thickness.reshape(levels, -1)
    flat_fields = fields.reshape(field_count, levels, -1)
    top_edges = jnp.cumsum(flat_thick, axis=0) - flat_thick
    surface = jnp.sum(flat_thick, axis=0)
    sigma_edges = (jnp.cumsum(weights) / jnp.sum(weights))[:, None]
    targets = surface[None] * sigma_edges
    previous = jnp.concatenate([jnp.zeros_like(targets[:1]), targets[:-1]], axis=0)
    edge_values = ppm_edges(flat_fields)
    left_edge = edge_values[:, :-1]
    curvature = 6.0 * (flat_fields - 0.5 * (left_edge + edge_values[:, 1:]))
    linear = edge_values[:, 1:] - left_edge + curvature

    def mass_block(edge_block):
        fraction = jnp.clip((edge_block[:, None] - top_edges[None]) / flat_thick[None], 0.0, 1.0)
        collected = []
        for member in range(field_count):
            partial_value = fraction * (
                left_edge[member][None]
                + fraction * (0.5 * linear[member][None] - fraction * curvature[member][None] / 3.0)
            )
            collected.append(jnp.sum(flat_thick[None] * partial_value, axis=1))
        return tuple(collected)

    grouped = targets.reshape(levels // 8, 8, -1)
    masses = lax.map(mass_block, grouped)
    results = []
    for mass in masses:
        mass_below = mass.reshape(levels, -1)
        mass_above = jnp.concatenate([jnp.zeros_like(mass_below[:1]), mass_below[:-1]], axis=0)
        results.append((mass_below - mass_above) / (targets - previous))
    return jnp.stack(results).reshape(fields.shape)


def modes_table(first_wave, wave_count, lon_count):
    wavenumber = first_wave + lax.iota(jnp.int32, wave_count)
    position = lax.iota(jnp.int32, lon_count)
    phase_index = wavenumber[:, None] * position[None, :] % lon_count
    angles = phase_index.astype(jnp.float32) * (2.0 * math.pi / lon_count)
    return (jnp.concatenate([jnp.cos(angles), jnp.sin(angles)], axis=0), wavenumber)


def weighted_spectrum(vectors, limits, modes, wavenumber):
    lon_count = vectors.shape[-1]
    spectrum = jnp.einsum("vi,ki->vk", vectors, modes, precision=HIGHEST)
    factor = jnp.where(wavenumber == 0, 1.0, 2.0) / lon_count
    kept_weight = jnp.where(wavenumber[None, :] <= limits[:, None], factor[None, :], 0.0)
    kept_weight = jnp.concatenate([kept_weight, kept_weight], axis=1)
    return spectrum * kept_weight


def filter_part(vectors, limits, first_wave, wave_count):
    modes, wavenumber = modes_table(first_wave, wave_count, vectors.shape[-1])
    weighted = weighted_spectrum(vectors, limits, modes, wavenumber)
    return jnp.dot(weighted, modes, precision=HIGHEST, preferred_element_type=jnp.float32)


def add_terms(earlier, later):
    return earlier + later


def local(zonal_wind, merid_wind, thickness, potential_temp, cutoff, sigma_weights):
    levels_dev, rows_dev, lon_count = zonal_wind.shape
    band_count = lax.axis_size("lat")
    band_index = lax.axis_index("lat")
    polar_rows = POLAR_BANDS * rows_dev
    all_rows = band_count * rows_dev
    wind_pair = jnp.stack([zonal_wind, merid_wind])
    southern = band_index < POLAR_BANDS
    is_polar = jnp.logical_or(southern, band_index >= band_count - POLAR_BANDS)
    offset = jnp.where(
        southern, band_index * rows_dev, band_index * rows_dev - all_rows + 2 * polar_rows
    )
    offset = jnp.clip(offset, 0, 2 * polar_rows - rows_dev)
    own_limits = lax.dynamic_slice_in_dim(cutoff, offset, rows_dev)
    limits = jnp.broadcast_to(own_limits, (2, levels_dev, rows_dev)).reshape(-1)

    def smoothed(wind_block):
        flat_rows = wind_block.reshape(-1, lon_count)
        return filter_part(flat_rows, limits, 0, KMAX).reshape(wind_block.shape)

    def unchanged(wind_block):
        return wind_block

    wind_pair = lax.cond(is_polar, smoothed, unchanged, wind_pair)
    zonal = wind_pair[0]
    stacked = jnp.stack([thickness, wind_pair[1], potential_temp])
    padded = with_halo(stacked, (("lat", 2),), 1)
    new_thick, new_temp = advance(thickness, potential_temp, zonal, padded[1], padded[0], padded[2])
    own_mass = jnp.sum(new_thick, axis=0)
    upper_mass = prefix(own_mass, "lev", add_terms, jnp.zeros_like(own_mass))
    mid_pressure = upper_mass[None] + jnp.cumsum(new_thick, axis=0) - 0.5 * new_thick
    new_zonal = pressure_push(zonal, mid_pressure)
    outgoing = jnp.stack([new_zonal, new_temp, new_thick])
    columns = lax.all_to_all(outgoing, "lev", split_axis=3, concat_axis=1, tiled=True)
    result = remap_columns(columns[:2], columns[2], sigma_weights)
    return (result[0], result[1])


def solution(mesh):
    in_specs = (
        P("lev", "lat", None),
        P("lev", "lat", None),
        P("lev", "lat", None),
        P("lev", "lat", None),
        P(),
        P(),
    )
    out_specs = (P(None, "lat", "lev"), P(None, "lat", "lev"))
    return jax.shard_map(local, mesh=mesh, in_specs=in_specs, out_specs=out_specs, check_vma=False)
```

profile of v0, /device:TPU:32, one launch (start us, length us, event | category | flops | bytes accessed | tf_op | source)
XLA Modules:
  0.0 282.6 jit_solution(11586409146098346025)
XLA Ops:
  7.2 2.0 pad_maximum_fusion.11
  9.3 1.2 slice_bitcast_fusion.9
  10.5 1.3 pad_maximum_fusion.14
  11.8 1.9 collective-permute-start
  13.8 27.1 %collective-permute-start.1 = (f32[3,4,1,2880]{3,1,2,0:T(4,128)S(1)}, f32[3,4,1,2880]{3,1,2,0:T(4,128)S(1)}, u32[]{:S(2)}, u32[]{:S(2)}) collective-permute-start(f32[3,4,1,2880]{3,1,2,0:T(4,128)S(1)} %copy.84), channel_id=1, source_target_pairs={{16,0},{32,16},{48,32},{64,48},{80,64},{96,80},{112,96},{128,112},... | collective-permute-start | bytes 414728 | tf_op jit(solution)/shard_map/ppermute | solution.py:25
  41.2 1.4 fusion.36
  44.4 0.8 fusion.37
  45.4 62.9 %all-gather.3.cloned.1.call-done = f32[128,2880]{1,0:T(8,128)} async-done(((f32[8,2880]{1,0:T(8,128)}), f32[128,2880]{1,0:T(8,128)}) %all-gather.3.cloned.1.call-update) | async-done | bytes 1474576 | tf_op jit(solution)/shard_map/all_gather | solution.py:32
  108.4 2.4 fusion.15
  111.0 1.2 fusion.35
  112.3 12.1 %copy.79 = f32[3,4,8,2880]{2,1,0,3:T(4,128)} copy(f32[3,4,8,2880]{3,2,1,0:T(8,128)S(1)} %pad_maximum_fusion.8) | data formatting | bytes 2211840 | tf_op jit(solution)/shard_map/stack | solution.py:177
  124.4 22.8 %reshape.137 = f32[16,1,17280]{2,1,0:T(1,128)} reshape(f32[2880,3,4,8]{3,2,1,0:T(4,128)} %bitcast.101) | data formatting | bytes 2211840
  147.2 18.2 %all-to-all-start = ((f32[16,1,17280]{2,1,0:T(1,128)}), f32[16,1,17280]{2,1,0:T(1,128)S(1)}, u32[]{:S(2)}, u32[]{:S(2)}) async-start(f32[16,1,17280]{2,1,0:T(1,128)} %reshape.137), calls=%async_computation | async-start | bytes 2211840 | tf_op jit(solution)/shard_map/all_to_all | solution.py:178
  166.2 0.8 divide_reduce_fusion
  167.0 14.3 %all-to-all-done = f32[16,1,17280]{2,1,0:T(1,128)S(1)} async-done(((f32[16,1,17280]{2,1,0:T(1,128)}), f32[16,1,17280]{2,1,0:T(1,128)S(1)}, u32[]{:S(2)}, u32[]{:S(2)}) %all-to-all-start) | async-done | bytes 1105952 | tf_op jit(solution)/shard_map/all_to_all | solution.py:178
  181.9 3.3 %reduce.4 = f32[16,17280]{1,0:T(8,128)S(1)} reduce(f32[16,1,17280]{2,1,0:T(1,128)S(1)} %all-to-all-done, f32[]{:T(128)} %broadcast.115), dimensions={1}, to_apply=%all_to_all.11.reduce_sub_computation | reduce | bytes 2211844 | tf_op jit(solution)/shard_map/all_to_all | solution.py:178
  185.2 27.2 %reshape.138 = f32[2880,3,4,8]{3,2,1,0:T(4,128)} reshape(f32[16,17280]{1,0:T(8,128)S(1)} %reduce.4) | data formatting | bytes 2211840
  212.4 12.9 %copy.80 = f32[3,4,8,16,180]{4,2,1,3,0:T(8,128)S(1)} copy(f32[3,4,8,16,180]{2,1,0,4,3:T(4,128)} %bitcast.100) | data formatting | bytes 2211840 | tf_op jit(solution)/shard_map/all_to_all | solution.py:178
  225.3 1.1 slice.252
  226.3 1.6 reshape.131
  228.4 0.9 slice_reduce_fusion
  229.7 1.3 reshape_squeeze.3
  231.0 1.1 reduce_window_sum.30
  232.1 1.0 sub.102
  233.2 0.9 broadcast_multiply_fusion
  234.1 0.8 broadcast_multiply_fusion.1
  234.9 1.3 mul.381
  236.2 35.5 %while.24 = (s32[]{:T(128)}, f32[8,8,1440]{2,1,0:T(8,128)}, f32[8,8,1440]{2,1,0:T(8,128)}, f32[1,64,8,180]{3,2,1,0:T(8,128)}, f32[8,8,1440]{2,1,0:T(8,128)}, /*i...) while((s32[]{:T(128)}, f32[8,8,1440]{2,1,0:T(8,128)}, ...), condition=%wide.wide.region_13.14_spmd, body=%wide.wide.region_10.13_spmd.sunk | while | flops 14169602 | bytes 7794801 | solution.py:109
  236.3 0.8 dynamic-slice_bitcast_fusion.3
  237.2 2.2 multiply_reduce_fusion.4
  239.4 0.6 bitcast_dynamic-update-slice_fusion.7
  240.8 0.8 dynamic-slice_bitcast_fusion.3
  241.6 2.2 multiply_reduce_fusion.4
  245.2 0.8 dynamic-slice_bitcast_fusion.3
  246.1 2.2 multiply_reduce_fusion.4
  249.6 0.8 dynamic-slice_bitcast_fusion.3
  250.5 2.2 multiply_reduce_fusion.4
  254.1 0.8 dynamic-slice_bitcast_fusion.3
  255.0 2.2 multiply_reduce_fusion.4
  258.5 0.8 dynamic-slice_bitcast_fusion.3
  259.4 2.2 multiply_reduce_fusion.4
  263.0 0.8 dynamic-slice_bitcast_fusion.3
  263.8 2.2 multiply_reduce_fusion.4
  267.4 0.8 dynamic-slice_bitcast_fusion.3
  268.3 2.2 multiply_reduce_fusion.4
  271.7 1.7 subtract_divide_fusion
  273.4 1.2 squeeze.28
  274.6 1.2 squeeze.29
  (77 shorter events, 15.9 us)
Async XLA Ops:
  7.2 101.2 %all-gather.3.cloned.1.call-start = ((), (), s32[]{:S(2)}) async-start(), calls=%async_computation.1 | async-start | bytes 1601536 | tf_op jit(solution)/shard_map/all_gather | solution.py:32
  9.3 1.2 copy-start.1
  9.3 31.6 %copy-start.2 = (f32[4,8,2880]{2,1,0:T(8,128)S(1)}, f32[4,8,2880]{2,1,0:T(8,128)}, u32[]{:S(2)}) copy-start(f32[4,8,2880]{2,1,0:T(8,128)} %param.15) | copy-start | bytes 1105924
  11.8 30.8 %collective-permute-start = (f32[3,4,1,2880]{3,1,2,0:T(4,128)S(1)}, f32[3,4,1,2880]{3,1,2,0:T(4,128)S(1)}, u32[]{:S(2)}, u32[]{:S(2)}) collective-permute-start(f32[3,4,1,2880]{3,1,2,0:T(4,128)S(1)} %copy.83), channel_id=1, source_target_pairs={{0,16},{16,32},{32,48},{48,64},{64,80},{80,96},{96,112},{112,128},... | collective-permute-start | bytes 414728 | tf_op jit(solution)/shard_map/ppermute | solution.py:24
  13.8 29.5 %collective-permute-start.1 = (f32[3,4,1,2880]{3,1,2,0:T(4,128)S(1)}, f32[3,4,1,2880]{3,1,2,0:T(4,128)S(1)}, u32[]{:S(2)}, u32[]{:S(2)}) collective-permute-start(f32[3,4,1,2880]{3,1,2,0:T(4,128)S(1)} %copy.84), channel_id=1, source_target_pairs={{16,0},{32,16},{48,32},{64,48},{80,64},{96,80},{112,96},{128,112},... | collective-permute-start | bytes 414728 | tf_op jit(solution)/shard_map/ppermute | solution.py:25
  124.4 41.0 %copy-start.3 = (f32[64]{0:T(128)S(1)}, f32[64]{0:T(128)}, u32[]{:S(2)}) copy-start(f32[64]{0:T(128)} %param.17) | copy-start | bytes 772
  147.2 34.2 %all-to-all-start = ((f32[16,1,17280]{2,1,0:T(1,128)}), f32[16,1,17280]{2,1,0:T(1,128)S(1)}, u32[]{:S(2)}, u32[]{:S(2)}) async-start(f32[16,1,17280]{2,1,0:T(1,128)} %reshape.137), calls=%async_computation | async-start | bytes 2211840 | tf_op jit(solution)/shard_map/all_to_all | solution.py:178
Sparse Core Ops, SparseCore 0:
  45.3 63.0 all-gather.2
where the time goes:
time: 284 us; the launch traced here: 283 us
  local copies, waits for them, and re-layouts  103 us (36%)
  waiting for transfers between devices  77.7 us (27%)
  starting transfers between devices  47.2 us (17%)
  other arithmetic  40.5 us (14%)
  between operations  14.3 us (5%)
    all_gather x1, waiting for transfers between devices, prefix(): gathered = lax.all_gather(part, axis)  62.9 us
    unnamed x10, local copies, waits for them, and re-layouts  50.1 us
    ppermute x1, starting transfers between devices, with_halo(): after = lax.ppermute(first, axis, down)  27.1 us
    all_to_all x1, starting transfers between devices, local(): lax.all_to_all(outgoing, 'lev', split_axis=3, concat_axis=1, tiled=True)  18.2 us
    reduce_sum x8, other arithmetic, mass_block(): collected.append(jnp.sum(flat_thick[None] * partial_value, axis=1))  17.5 us
    all_to_all x1, waiting for transfers between devices, local(): lax.all_to_all(outgoing, 'lev', split_axis=3, concat_axis=1, tiled=True)  14.3 us
    all_to_all x2, local copies, waits for them, and re-layouts, local(): lax.all_to_all(outgoing, 'lev', split_axis=3, concat_axis=1, tiled=True)  13.4 us
    another operation x1, local copies, waits for them, and re-layouts, local(): outgoing = jnp.stack([new_zonal, new_temp, new_thick])  12.1 us
  transfers between devices with their start and end apart: 4, of which 3 were waited for; matrix products, arithmetic and copies ran while one was open for 1% of the time, Pallas kernels for 0%

commit v1 on v0

v1 whole, which is shorter than its diff:
```python
import functools
import math

import jax
import jax.numpy as jnp
import numpy as np
from jax import lax
from jax.experimental import pallas as pl
from jax.experimental.pallas import tpu as pltpu
from jax.sharding import PartitionSpec as P

F32 = jnp.float32
BF16 = jnp.bfloat16

LON = 2880
EXT = 2944
CHUNKS = EXT // 128
LEVELS = 64
ROWS = 8
LEV_DEV = 4
BANDS = 32
PEERS = 16
PIECE = LON // PEERS
TAIL = PIECE - 128
RADIX = 5
PART = LON // RADIX
POLAR = 16
COURANT = 0.02
PRESSURE_COEF = 0.05
VEC = 80


def mode_table():
    j = np.arange(64)
    orders = [[5 * j], [5 * j + 1, 5 * j + 4], [5 * j + 2, 5 * j + 3]]
    r = np.arange(PART)
    columns = []
    for order in orders:
        waves = np.concatenate(order)
        angle = 2.0 * np.pi * ((r[:, None] * waves[None, :]) % LON) / LON
        columns += [np.cos(angle), np.sin(angle)]
    table = np.concatenate(columns, axis=1)
    high = table.astype(np.float32).astype(jnp.bfloat16)
    low = (table - high.astype(np.float64)).astype(np.float32).astype(jnp.bfloat16)
    return high, low


def split(x):
    high = x.astype(BF16)
    low = (x - high.astype(F32)).astype(BF16)
    return high, low


def dot3(x, high_ref, low_ref, first, count, transposed):
    dims = (((1,), (1,)), ((), ())) if transposed else (((1,), (0,)), ((), ()))
    x_high, x_low = split(x)
    t_high = high_ref[:, first : first + count]
    t_low = low_ref[:, first : first + count]
    dot = functools.partial(lax.dot_general, dimension_numbers=dims, preferred_element_type=F32)
    return dot(x_high, t_high) + (dot(x_low, t_high) + dot(x_high, t_low))


def spin(x, shift):
    shift = shift % 128
    return x if shift == 0 else pltpu.roll(x, shift, axis=1)


def filter_rows(x_ref, high_ref, low_ref, limit):
    c1, c2 = math.cos(2 * math.pi / 5), math.cos(4 * math.pi / 5)
    s1, s2 = math.sin(2 * math.pi / 5), math.sin(4 * math.pi / 5)
    x = [x_ref[:, PART * q : PART * (q + 1)] for q in range(RADIX)]
    sum1, dif1 = x[1] + x[4], x[1] - x[4]
    sum2, dif2 = x[2] + x[3], x[2] - x[3]
    z0 = x[0] + sum1 + sum2
    z1 = jnp.concatenate([x[0] + c1 * sum1 + c2 * sum2, s1 * dif1 + s2 * dif2], axis=0)
    z2 = jnp.concatenate([x[0] + c2 * sum1 + c1 * sum2, s2 * dif1 - s1 * dif2], axis=0)
    lane = lax.broadcasted_iota(jnp.int32, (VEC, 128), 1)
    half = lane < 64
    slot = jnp.where(half, lane, lane - 64)
    sign = jnp.where(half, 1.0, -1.0).astype(F32)

    wave0 = 5 * slot
    weight0 = jnp.where(wave0 <= limit, jnp.where(wave0 == 0, 1.0 / LON, 2.0 / LON), 0.0)
    spec0 = dot3(z0, high_ref, low_ref, 0, 128, False) * weight0
    back0 = dot3(spec0, high_ref, low_ref, 0, 128, True)
    backs = []
    for z, first, low_wave, high_wave in ((z1, 128, 1, 4), (z2, 384, 2, 3)):
        wave = 5 * slot + jnp.where(half, low_wave, high_wave)
        weight = jnp.where(wave <= limit, 2.0 / LON, 0.0)
        flip = weight * sign
        y = dot3(z, high_ref, low_ref, first, 256, False)
        cc, cs = y[:VEC, :128], y[:VEC, 128:]
        sc, ss = y[VEC:, :128], y[VEC:, 128:]
        a = cc - sign * ss
        b = cs + sign * sc
        even = jnp.concatenate([a * weight, b * weight], axis=1)
        odd = jnp.concatenate([b * flip, -(a * flip)], axis=1)
        back = dot3(jnp.concatenate([even, odd], axis=0), high_ref, low_ref, first, 256, True)
        backs += [back[:VEC], back[VEC:]]
    e1, o1, e2, o2 = backs
    out = [back0 + e1 + e2]
    p, m = back0 + c1 * e1 + c2 * e2, s1 * o1 + s2 * o2
    r, n = back0 + c2 * e1 + c1 * e2, s2 * o1 - s1 * o2
    return out + [p + m, r + n, r - n, p - m]


def dynamics_kernel(
    band_ref, cutoff_ref, u_ref, v_ref, h_ref, t_ref, south_ref, north_ref, high_ref, low_ref,
    out_ref, x_ref, y_ref, e_ref, halo_ref, n_ref,
):
    band = band_ref[0]
    lane = lax.broadcasted_iota(jnp.int32, (8, 128), 1)
    row = lax.broadcasted_iota(jnp.int32, (8, 128), 0)
    south_row = band * ROWS - 1
    north_row = band * ROWS + ROWS
    total_rows = BANDS * ROWS

    def is_polar(r):
        return jnp.logical_and(
            jnp.logical_and(r >= 0, r < total_rows),
            jnp.logical_or(r < POLAR, r >= total_rows - POLAR),
        )

    def entry(r):
        index = jnp.where(r < POLAR, r, r - (total_rows - 2 * POLAR))
        return cutoff_ref[jnp.clip(index, 0, 2 * POLAR - 1)]

    own = is_polar(band * ROWS)
    south = is_polar(south_row)
    north = is_polar(north_row)

    for f, ref in enumerate((u_ref, v_ref, h_ref, t_ref)):
        e_ref[f, :, :, 0:LON] = ref[...]
    for f in range(3):
        halo_ref[f, 0:4, 0:LON] = south_ref[f]
        halo_ref[f, 4:8, 0:LON] = north_ref[f]

    @pl.when(jnp.logical_or(own, jnp.logical_or(south, north)))
    def _():
        x_ref[0:32, :] = u_ref[...].reshape(32, LON)
        x_ref[32:64, :] = v_ref[...].reshape(32, LON)
        x_ref[64:68, :] = south_ref[0]
        x_ref[68:72, :] = north_ref[0]
        x_ref[72:80, :] = jnp.zeros((8, LON), F32)
        own_limit = jnp.zeros((8, 128), jnp.int32)
        for r in range(ROWS):
            own_limit = jnp.where(row == r, entry(band * ROWS + r), own_limit)
        halo_limit = jnp.where(row < 4, entry(south_row), entry(north_row))
        limit = jnp.concatenate([own_limit] * 8 + [halo_limit] * 2, axis=0)
        pieces = filter_rows(x_ref, high_ref, low_ref, limit)
        for q in range(RADIX):
            y_ref[:, PART * q : PART * (q + 1)] = pieces[q]

        @pl.when(own)
        def _():
            e_ref[0, :, :, 0:LON] = y_ref[0:32, :].reshape(4, 8, LON)
            e_ref[1, :, :, 0:LON] = y_ref[32:64, :].reshape(4, 8, LON)

        @pl.when(south)
        def _():
            halo_ref[0, 0:4, 0:LON] = y_ref[64:68, :]

        @pl.when(north)
        def _():
            halo_ref[0, 4:8, 0:LON] = y_ref[68:72, :]

    def wrap(ref, index):
        last = ref[index + (slice(None), slice(EXT - 128, EXT))]
        first = ref[index + (slice(None), slice(0, 128))]
        ref[index + (slice(None), slice(EXT - 128, EXT))] = jnp.where(
            lane < 64, last, jnp.where(lane < 96, spin(first, 64), spin(last, 64))
        )

    for f in range(4):
        for l in range(LEV_DEV):
            wrap(e_ref, (f, l))
    for f in range(3):
        wrap(halo_ref, (f,))

    scale = COURANT * 0.25
    for l in range(LEV_DEV):

        def load(f, i):
            return e_ref[f, l, :, 128 * i : 128 * (i + 1)]

        def side(f, r, i):
            return jnp.broadcast_to(halo_ref[f, r : r + 1, 128 * i : 128 * (i + 1)], (8, 128))

        i = CHUNKS - 1
        u, h = load(0, i), load(2, i)
        q = h * load(3, i)
        before = tuple(spin(z, 1) for z in (u, h, q))
        flux = {}
        state = {}
        for i in range(CHUNKS + 1):
            if i < CHUNKS:
                u, v, h = load(0, i), load(1, i), load(2, i)
                q = h * load(3, i)
                now = tuple(spin(z, 1) for z in (u, h, q))
                ul, hl, ql = (jnp.where(lane == 0, b, n) for b, n in zip(before, now))
                before = now
                face = u + ul
                fh, fq = face * (h + hl), face * (q + ql)
                turned = (spin(fh, -1), spin(fq, -1))
                if i == 0:
                    first = turned
                vs, hs = side(0, l, i), side(1, l, i)
                qs = hs * side(2, l, i)
                vn, hn = side(0, 4 + l, i), side(1, 4 + l, i)
                qn = hn * side(2, 4 + l, i)
                vm, hm, qm = (
                    jnp.where(row == 0, s, pltpu.roll(z, 1, axis=0))
                    for s, z in ((vs, v), (hs, h), (qs, q))
                )
                vp, hp, qp = (
                    jnp.where(row == 7, s, pltpu.roll(z, 7, axis=0))
                    for s, z in ((vn, v), (hn, h), (qn, q))
                )
                wm, wp = v + vm, v + vp
                gh = wp * (h + hp) - wm * (h + hm) - fh
                gq = wp * (q + qp) - wm * (q + qm) - fq
                state[i] = (h, q, gh, gq)
                flux[i] = turned
            if i >= 1:
                k = i - 1
                nxt = flux[i] if i < CHUNKS else first
                h0, q0, gh0, gq0 = state.pop(k)
                mine = flux.pop(k)
                rh = jnp.where(lane == 127, nxt[0], mine[0])
                rq = jnp.where(lane == 127, nxt[1], mine[1])
                new_h = h0 - scale * (rh + gh0)
                new_q = q0 - scale * (rq + gq0)
                n_ref[0, l, :, 128 * k : 128 * (k + 1)] = new_h
                n_ref[1, l, :, 128 * k : 128 * (k + 1)] = new_q / new_h

    def fetch(f, l, i):
        if f == 0:
            return e_ref[0, l, :, 128 * i : 128 * (i + 1)]
        return n_ref[2 - f, l, :, 128 * i : 128 * (i + 1)]

    for j in range(PEERS):
        for f in range(3):
            for pair in range(2):
                tails = []
                for l in (2 * pair, 2 * pair + 1):
                    start = PIECE * j
                    i, off = start // 128, start % 128
                    if off == 0:
                        slab = fetch(f, l, i)
                    else:
                        slab = jnp.where(
                            lane < 128 - off,
                            spin(fetch(f, l, i), -off),
                            spin(fetch(f, l, i + 1), -off),
                        )
                    out_ref[j, f * 4 + l] = slab
                    start = PIECE * j + 128
                    i, off = start // 128, start % 128
                    target = 64 * (l % 2)
                    tail = spin(fetch(f, l, i), target - off)
                    if off > 64:
                        other = spin(fetch(f, l, i + 1), target - off)
                        tail = jnp.where(lane < target + 128 - off, tail, other)
                    tails.append(tail)
                packed = jnp.where(lane < 64, tails[0], tails[1])
                if f == 2:
                    at = (PIECE * j - 1) % LON
                    i, off = at // 128, at % 128
                    packed = jnp.where(
                        lane == 127,
                        spin(fetch(f, 2 * pair, i), 127 - off),
                        jnp.where(lane == 63, spin(fetch(f, 2 * pair + 1, i), 63 - off), packed),
                    )
                out_ref[j, 12 + f * 2 + pair] = packed


EDGE, THICK, AU, BU, CU, AT, BT, CT, FU, FT = range(10)
BLOCK = 8


def remap_kernel(sigma_ref, inverse_ref, r_ref, wind_ref, temp_ref, s_ref, f_ref, a_ref, lo_ref, hi_ref):
    lane = lax.broadcasted_iota(jnp.int32, (8, 128), 1)
    left = lane < 64
    zero = jnp.zeros((8, 128), F32)

    def turn(x):
        return pltpu.roll(x, 64, axis=1)

    def twice(p, o, odd):
        return jnp.where(left, o, p) if odd else jnp.where(left, p, o)

    def unpack(s, carry):
        ea, eb, ed, fua, fub, fta, ftb = carry
        for l in range(LEV_DEV):
            k = s * LEV_DEV + l
            odd = l % 2
            ua, ta, ha = r_ref[s, l], r_ref[s, 4 + l], r_ref[s, 8 + l]
            packs = [r_ref[s, 12 + 2 * f + l // 2] for f in range(3)]
            turns = [turn(p) for p in packs]
            ub, tb, hb = (o if odd else p for p, o in zip(packs, turns))
            td = twice(packs[1], turns[1], odd)
            hd = twice(packs[2], turns[2], odd)
            pa = ea + 0.5 * ha
            pb = eb + 0.5 * hb
            ra, rb = pltpu.roll(pa, 1, axis=1), pltpu.roll(pb, 1, axis=1)
            la, lb = pltpu.roll(pa, 127, axis=1), pltpu.roll(pb, 127, axis=1)
            wa = jnp.where(lane == 127, lb, la) - jnp.where(lane == 0, rb, ra)
            wb = lb - jnp.where(lane == 0, ra, rb)
            ua = ua - PRESSURE_COEF * wa
            ub = ub - PRESSURE_COEF * wb
            ud = jnp.where(left, ub, turn(ub))
            s_ref[EDGE, k, 0], s_ref[EDGE, k, 1] = ea, ed
            s_ref[THICK, k, 0], s_ref[THICK, k, 1] = ha, hd
            s_ref[FU, k, 0], s_ref[FU, k, 1] = fua, fub
            s_ref[FT, k, 0], s_ref[FT, k, 1] = fta, ftb
            f_ref[0, k, 0], f_ref[0, k, 1] = ua, ud
            f_ref[1, k, 0], f_ref[1, k, 1] = ta, td
            ea, eb, ed = ea + ha, eb + hb, ed + hd
            fua, fub = fua + ha * ua, fub + hd * ud
            fta, ftb = fta + ha * ta, ftb + hd * td
        return ea, eb, ed, fua, fub, fta, ftb

    sums = lax.fori_loop(0, PEERS, unpack, (zero,) * 7)
    surface = (sums[0], sums[2])
    inverse = tuple(1.0 / s for s in surface)

    for m in range(2):
        a_ref[m, 0] = f_ref[m, 0]
        a_ref[m, 1] = 0.5 * (f_ref[m, 0] + f_ref[m, 1])
        a_ref[m, LEVELS - 1] = 0.5 * (f_ref[m, LEVELS - 2] + f_ref[m, LEVELS - 1])
        a_ref[m, LEVELS] = f_ref[m, LEVELS - 1]

    def edges(k, _):
        for m in range(2):
            a_ref[m, k] = (7.0 / 12.0) * (f_ref[m, k - 1] + f_ref[m, k]) - (1.0 / 12.0) * (
                f_ref[m, k - 2] + f_ref[m, k + 1]
            )
        return 0

    lax.fori_loop(2, LEVELS - 1, edges, 0)

    def coefficients(k, _):
        rd = 1.0 / s_ref[THICK, k]
        rd2 = rd * rd
        for m, (pa, pb, pc) in enumerate(((AU, BU, CU), (AT, BT, CT))):
            a0, a1, f = a_ref[m, k], a_ref[m, k + 1], f_ref[m, k]
            c = 6.0 * (f - 0.5 * (a0 + a1))
            s_ref[pa, k] = a0
            s_ref[pb, k] = (0.5 * rd) * (a1 - a0 + c)
            s_ref[pc, k] = (rd2 * (-1.0 / 3.0)) * c
        return 0

    lax.fori_loop(0, LEVELS, coefficients, 0)

    blocks = LEVELS // BLOCK
    bounds = [
        tuple(s * sigma_ref[BLOCK * b - 1] for s in surface) for b in range(1, blocks)
    ]

    def count(k, carry):
        ea, eb = s_ref[EDGE, k, 0], s_ref[EDGE, k, 1]
        out = []
        for (pa, pb), (ca, cb) in zip(bounds, carry):
            out.append((ca + jnp.where(ea <= pa, 1.0, 0.0), cb + jnp.where(eb <= pb, 1.0, 0.0)))
        return tuple(out)

    counts = lax.fori_loop(1, LEVELS, count, tuple((zero, zero) for _ in bounds))
    lo_ref[0] = 0
    hi_ref[blocks - 1] = LEVELS
    for b, (ca, cb) in enumerate(counts):
        lo_ref[b + 1] = jnp.min(jnp.minimum(ca, cb)).astype(jnp.int32)
        hi_ref[b] = jnp.max(jnp.maximum(ca, cb)).astype(jnp.int32) + 1

    def block(b, carry):
        low, high = lo_ref[b], hi_ref[b]
        base = b * BLOCK
        pa = [surface[0] * sigma_ref[base + i] for i in range(BLOCK)]
        pb = [
            surface[1] * jnp.where(left, sigma_ref[base + 2 * i], sigma_ref[base + 2 * i + 1])
            for i in range(BLOCK // 2)
        ]
        places = [(p, 0) for p in pa] + [(p, 1) for p in pb]
        start = []
        for p, part in places:
            start += [s_ref[FU, low, part], s_ref[FT, low, part]]

        def layer(k, sums):
            out = []
            for part in range(2):
                e, d, au, bu, cu, at, bt, ct = (s_ref[plane, k, part] for plane in range(8))
                for n, (p, where) in enumerate(places):
                    if where == part:
                        y = jnp.minimum(jnp.maximum(p - e, 0.0), d)
                        out.append(sums[2 * n] + y * (au + y * (bu + y * cu)))
                        out.append(sums[2 * n + 1] + y * (at + y * (bt + y * ct)))
            return tuple(out)

        mass = lax.fori_loop(low, high, layer, tuple(start))
        following = []
        for m, out_ref in enumerate((wind_ref, temp_ref)):
            last_a, last_b = carry[2 * m], carry[2 * m + 1]
            for i in range(BLOCK):
                here = mass[2 * i + m]
                factor = inverse[0] * inverse_ref[base + i]
                out_ref[base + i, :, 0:128] = (here - last_a) * factor
                last_a = here
            for i in range(BLOCK // 2):
                here = mass[2 * (BLOCK + i) + m]
                turned = turn(here)
                factor = inverse[1] * jnp.where(
                    left, inverse_ref[base + 2 * i], inverse_ref[base + 2 * i + 1]
                )
                value = (here - jnp.where(left, last_b, turned)) * factor
                out_ref[base + 2 * i, :, 128:PIECE] = value[:, 0:TAIL]
                out_ref[base + 2 * i + 1, :, 128:PIECE] = turn(value)[:, 0:TAIL]
                last_b = turned
            following += [last_a, last_b]
        return tuple(following)

    lax.fori_loop(0, blocks, block, (zero,) * 4)


def whole(space=pltpu.VMEM):
    return pl.BlockSpec(memory_space=space)


def local(zonal_wind, merid_wind, thickness, potential_temp, cutoff, sigma_weights):
    band = lax.axis_index("lat").astype(jnp.int32).reshape(1)
    up = [(i, i + 1) for i in range(BANDS - 1)]
    down = [(i + 1, i) for i in range(BANDS - 1)]
    fields = (merid_wind, thickness, potential_temp)
    south = lax.ppermute(jnp.stack([f[:, ROWS - 1] for f in fields]), "lat", up)
    north = lax.ppermute(jnp.stack([f[:, 0] for f in fields]), "lat", down)
    high, low = mode_table()
    outgoing = pl.pallas_call(
        dynamics_kernel,
        name="dynamics",
        out_shape=jax.ShapeDtypeStruct((PEERS, 18, 8, 128), F32),
        in_specs=[whole(pltpu.SMEM)] * 2 + [whole()] * 8,
        out_specs=whole(),
        scratch_shapes=[
            pltpu.VMEM((VEC, LON), F32),
            pltpu.VMEM((VEC, LON), F32),
            pltpu.VMEM((4, LEV_DEV, ROWS, EXT), F32),
            pltpu.VMEM((3, 8, EXT), F32),
            pltpu.VMEM((2, LEV_DEV, ROWS, EXT), F32),
        ],
    )(
        band, cutoff, zonal_wind, merid_wind, thickness, potential_temp, south, north,
        jnp.asarray(high), jnp.asarray(low),
    )
    columns = lax.all_to_all(outgoing, "lev", split_axis=0, concat_axis=0, tiled=True)
    total = jnp.sum(sigma_weights)
    sigma = jnp.cumsum(sigma_weights) / total
    inverse = total / sigma_weights
    shape = jax.ShapeDtypeStruct((LEVELS, ROWS, PIECE), F32)
    return pl.pallas_call(
        remap_kernel,
        name="remap",
        out_shape=(shape, shape),
        in_specs=[whole(pltpu.SMEM)] * 2 + [whole()],
        out_specs=(whole(), whole()),
        scratch_shapes=[
            pltpu.VMEM((10, LEVELS, 2, 8, 128), F32),
            pltpu.VMEM((2, LEVELS, 2, 8, 128), F32),
            pltpu.VMEM((2, LEVELS + 1, 2, 8, 128), F32),
            pltpu.SMEM((LEVELS // BLOCK,), jnp.int32),
            pltpu.SMEM((LEVELS // BLOCK,), jnp.int32),
        ],
    )(sigma, inverse, columns)


def solution(mesh):
    field = P("lev", "lat", None)
    out = P(None, "lat", "lev")
    return jax.shard_map(
        local,
        mesh=mesh,
        in_specs=(field, field, field, field, P(), P()),
        out_specs=(out, out),
        check_vma=False,
    )
```

time: 284 us -> 68.3 us (0.24)
  the two profiles are of different devices: /device:TPU:32 before, /device:TPU:1 now
where the time goes in v1:
time: 68.3 us; the launch traced here: 67.9 us
  Pallas kernels  25.7 us (38%)
  waiting for transfers between devices  18.2 us (27%)
  starting transfers between devices  14.5 us (21%)
  local copies, waits for them, and re-layouts  5.51 us (8%)
  other arithmetic  3.27 us (5%)
  between operations  0.74 us (1%)
    all_to_all x1, waiting for transfers between devices, local(): lax.all_to_all(outgoing, 'lev', split_axis=0, concat_axis=0, tiled=True)  16.2 us
    pallas_call x1, Pallas kernels, local(): pl.pallas_call(remap_kernel, name='remap', out_shape=(shape, shape), in_s...  13 us
    pallas_call x1, Pallas kernels, local(): pl.pallas_call(dynamics_kernel, name='dynamics', out_shape=jax.ShapeDtype...  12.7 us
    ppermute x1, starting transfers between devices, local(): north = lax.ppermute(jnp.stack([f[:, 0] for f in fields]), 'lat', down)  8.75 us
    all_to_all x1, starting transfers between devices, local(): lax.all_to_all(outgoing, 'lev', split_axis=0, concat_axis=0, tiled=True)  3.83 us
    slice x3, local copies, waits for them, and re-layouts, local(): north = lax.ppermute(jnp.stack([f[:, 0] for f in fields]), 'lat', down)  3.65 us
    ppermute x1, waiting for transfers between devices, local(): south = lax.ppermute(jnp.stack([f[:, ROWS - 1] for f in fields]), 'lat', up)  2 us
    ppermute x1, starting transfers between devices, local(): south = lax.ppermute(jnp.stack([f[:, ROWS - 1] for f in fields]), 'lat', up)  1.92 us
  transfers between devices with their start and end apart: 3, of which 2 were waited for; matrix products, arithmetic and copies ran while one was open for 5% of the time, Pallas kernels for 0%

profile of v1, /device:TPU:1, one launch (start us, length us, event | category | flops | bytes accessed | tf_op | source)
XLA Modules:
  0.0 67.9 jit_solution(10501692475764064052)
XLA Ops:
  0.6 1.3 %fusion.1 = (f32[4,1,2880]{2,1,0:T(1,128)S(1)}, f32[4,1,2880]{2,1,0:T(1,128)S(1)}) fusion(f32[4,8,2880]{2,1,0:T(8,128)} %h_ref.1), kind=kLoop, calls=%fused_computation.11 | loop fusion | bytes 184320 | tf_op jit(solution)/shard_map/slice | solution.py:433
  1.9 1.2 %fusion.2 = (f32[4,1,2880]{2,1,0:T(1,128)S(1)}, f32[4,1,2880]{2,1,0:T(1,128)S(1)}) fusion(f32[4,8,2880]{2,1,0:T(8,128)} %t_ref.1), kind=kLoop, calls=%fused_computation.12 | loop fusion | bytes 184320 | tf_op jit(solution)/shard_map/slice | solution.py:433
  3.1 1.2 %fusion = (f32[4,1,2880]{2,1,0:T(1,128)S(1)}, f32[4,1,2880]{2,1,0:T(1,128)S(1)}) fusion(f32[4,8,2880]{2,1,0:T(8,128)} %v_ref.1), kind=kLoop, calls=%fused_computation.10 | loop fusion | bytes 184320 | tf_op jit(solution)/shard_map/slice | solution.py:433
  4.4 8.7 %collective-permute-start.1 = (f32[3,4,2880]{2,1,0:T(4,128)S(1)}, f32[3,4,2880]{2,1,0:T(4,128)S(1)}, u32[]{:S(2)}, u32[]{:S(2)}) collective-permute-start(f32[3,4,2880]{2,1,0:T(4,128)S(1)} %pad_maximum_fusion.1), channel_id=1, source_target_pairs={{16,0},{32,16},{48,32},{64,48},{80,64},{96,80},{112,96},{128,112},... | collective-permute-start | bytes 414728 | tf_op jit(solution)/shard_map/ppermute | solution.py:433
  13.2 1.9 %collective-permute-start = (f32[3,4,2880]{2,1,0:T(4,128)S(1)}, f32[3,4,2880]{2,1,0:T(4,128)S(1)}, u32[]{:S(2)}, u32[]{:S(2)}) collective-permute-start(f32[3,4,2880]{2,1,0:T(4,128)S(1)} %pad_maximum_fusion), channel_id=1, source_target_pairs={{0,16},{16,32},{32,48},{48,64},{64,80},{80,96},{96,112},{112,128},... | collective-permute-start | bytes 414728 | tf_op jit(solution)/shard_map/ppermute | solution.py:432
  15.2 0.0 collective-permute-done.1.north_ref
  15.2 0.0 copy-start.1
  15.2 2.0 %collective-permute-done.south_ref = f32[3,4,2880]{2,1,0:T(4,128)S(1)} collective-permute-done((f32[3,4,2880]{2,1,0:T(4,128)S(1)}, f32[3,4,2880]{2,1,0:T(4,128)S(1)}, u32[]{:S(2)}, u32[]{:S(2)}) %collective-permute-start) | collective-permute-done | bytes 138272 | tf_op jit(solution)/shard_map/ppermute | solution.py:432
  17.2 0.0 copy-start.2
  17.2 0.0 copy-done.1
  17.2 0.7 copy-done.2
  17.9 12.7 %dynamics.1 = f32[16,18,8,128]{3,2,1,0:T(8,128)} custom-call(s32[1]{0:T(128)} %bitcast.1.band_ref, s32[32]{0:T(128)} %cutoff_ref.1, f32[4,8,2880]{2,1,0:T(8,128)} %u_ref.1, f32[4,8,2880]{2,1,0:T(8,128)} %v_ref.1, f32[4,8,2880]{2,1,0:T(8,128)} %h_ref.1, f32[4,8,2880]{2,1,0:T(8,128)} %t_ref.1, f32[3,4,2880]{2,1,0:T(4,128)} %copy-done.2, ...), custom_call_target="tpu_custom_call" | custom-call | tf_op jit(solution)/shard_map/dynamics/pallas_call | solution.py:435
  30.6 0.0 copy-start.3
  30.6 3.8 %all-to-all-start = ((f32[16,18,8,128]{3,2,1,0:T(8,128)}), f32[16,18,8,128]{3,2,1,0:T(8,128)S(1)}, u32[]{:S(2)}, u32[]{:S(2)}) async-start(f32[16,18,8,128]{3,2,1,0:T(8,128)} %dynamics.1), calls=%async_computation | async-start | bytes 2359296 | tf_op jit(solution)/shard_map/all_to_all | solution.py:452
  34.4 0.0 copy-done.3
  34.4 0.6 reduce_sum.9
  35.0 0.1 copy.17
  35.1 0.1 reduce-window.9
  35.2 1.3 %divide_reduce_fusion.sigma_ref = f32[64]{0:T(128)} fusion(f32[64,1]{1,0:T(8,128)S(1)} %reduce-window.9, f32[]{:T(128)} %reduce_sum.9), kind=kLoop, calls=%fused_computation.8 | loop fusion | flops 64 | bytes 516 | tf_op jit(solution)/shard_map/div | solution.py:454
  36.6 1.2 %broadcast_divide_fusion.inverse_ref = f32[64]{0:T(128)} fusion(f32[64]{0:T(128)S(1)} %copy-done.3, f32[]{:T(128)} %reduce_sum.9), kind=kLoop, calls=%fused_computation.9 | loop fusion | flops 64 | bytes 516 | tf_op jit(solution)/shard_map/div | solution.py:455
  37.7 16.2 %all-to-all-done.r_ref = f32[16,18,8,128]{3,2,1,0:T(8,128)S(1)} async-done(((f32[16,18,8,128]{3,2,1,0:T(8,128)}), f32[16,18,8,128]{3,2,1,0:T(8,128)S(1)}, u32[]{:S(2)}, u32[]{:S(2)}) %all-to-all-start) | async-done | bytes 1179680 | tf_op jit(solution)/shard_map/all_to_all | solution.py:452
  54.0 0.0 copy-start
  54.0 1.0 %copy-done = f32[16,18,8,128]{3,2,1,0:T(8,128)} copy-done((f32[16,18,8,128]{3,2,1,0:T(8,128)}, f32[16,18,8,128]{3,2,1,0:T(8,128)S(1)}, u32[]{:S(2)}) %copy-start) | copy-done | bytes 1179672
  55.0 13.0 %remap.1 = (f32[64,8,180]{2,1,0:T(8,128)}, f32[64,8,180]{2,1,0:T(8,128)}) custom-call(f32[64]{0:T(128)} %divide_reduce_fusion.sigma_ref, f32[64]{0:T(128)} %broadcast_divide_fusion.inverse_ref, f32[16,18,8,128]{3,2,1,0:T(8,128)} %copy-done), custom_call_target="tpu_custom_call" | custom-call | tf_op jit(solution)/shard_map/remap/pallas_call | solution.py:457
  (6 shorter events, 0.2 us)
Async XLA Ops:
  4.4 10.8 %collective-permute-start.1 = (f32[3,4,2880]{2,1,0:T(4,128)S(1)}, f32[3,4,2880]{2,1,0:T(4,128)S(1)}, u32[]{:S(2)}, u32[]{:S(2)}) collective-permute-start(f32[3,4,2880]{2,1,0:T(4,128)S(1)} %pad_maximum_fusion.1), channel_id=1, source_target_pairs={{16,0},{32,16},{48,32},{64,48},{80,64},{96,80},{112,96},{128,112},... | collective-permute-start | bytes 414728 | tf_op jit(solution)/shard_map/ppermute | solution.py:433
  13.2 4.0 %collective-permute-start = (f32[3,4,2880]{2,1,0:T(4,128)S(1)}, f32[3,4,2880]{2,1,0:T(4,128)S(1)}, u32[]{:S(2)}, u32[]{:S(2)}) collective-permute-start(f32[3,4,2880]{2,1,0:T(4,128)S(1)} %pad_maximum_fusion), channel_id=1, source_target_pairs={{0,16},{16,32},{32,48},{48,64},{64,80},{80,96},{96,112},{112,128},... | collective-permute-start | bytes 414728 | tf_op jit(solution)/shard_map/ppermute | solution.py:432
  15.2 2.0 %copy-start.1 = (f32[3,4,2880]{2,1,0:T(4,128)}, f32[3,4,2880]{2,1,0:T(4,128)S(1)}, u32[]{:S(2)}) copy-start(f32[3,4,2880]{2,1,0:T(4,128)S(1)} %collective-permute-done.1.north_ref) | copy-start | bytes 414724
  17.2 0.7 copy-start.2
  30.6 3.8 %copy-start.3 = (f32[64]{0:T(128)S(1)}, f32[64]{0:T(128)}, u32[]{:S(2)}) copy-start(f32[64]{0:T(128)} %param.13) | copy-start | bytes 772
  30.6 23.4 %all-to-all-start = ((f32[16,18,8,128]{3,2,1,0:T(8,128)}), f32[16,18,8,128]{3,2,1,0:T(8,128)S(1)}, u32[]{:S(2)}, u32[]{:S(2)}) async-start(f32[16,18,8,128]{3,2,1,0:T(8,128)} %dynamics.1), calls=%async_computation | async-start | bytes 2359296 | tf_op jit(solution)/shard_map/all_to_all | solution.py:452
  54.0 1.0 %copy-start = (f32[16,18,8,128]{3,2,1,0:T(8,128)}, f32[16,18,8,128]{3,2,1,0:T(8,128)S(1)}, u32[]{:S(2)}) copy-start(f32[16,18,8,128]{3,2,1,0:T(8,128)S(1)} %all-to-all-done.r_ref) | copy-start | bytes 3538948

commit v2 on v0

v2 whole, which is shorter than its diff:
```python
import functools
import math

import jax
import jax.numpy as jnp
import numpy as np
from jax import lax
from jax.experimental import pallas as pl
from jax.experimental.pallas import tpu as pltpu
from jax.sharding import PartitionSpec as P

F32 = jnp.float32
BF16 = jnp.bfloat16

LON = 2880
EXT = 2944
CHUNKS = EXT // 128
LEVELS = 64
ROWS = 8
LEV_DEV = 4
BANDS = 32
PEERS = 16
PIECE = LON // PEERS
TAIL = PIECE - 128
RADIX = 5
PART = LON // RADIX
POLAR = 16
COURANT = 0.02
PRESSURE_COEF = 0.05


def mode_table():
    j = np.arange(64)
    orders = [[5 * j], [5 * j + 1, 5 * j + 4], [5 * j + 2, 5 * j + 3]]
    r = np.arange(PART)
    columns = []
    for order in orders:
        waves = np.concatenate(order)
        angle = 2.0 * np.pi * ((r[:, None] * waves[None, :]) % LON) / LON
        columns += [np.cos(angle), np.sin(angle)]
    table = np.concatenate(columns, axis=1)
    high = table.astype(np.float32).astype(jnp.bfloat16)
    low = (table - high.astype(np.float64)).astype(np.float32).astype(jnp.bfloat16)
    return np.stack([high, low])


def split(x):
    high = x.astype(BF16)
    low = (x - high.astype(F32)).astype(BF16)
    return high, low


def dot3(x, table_ref, first, count, transposed):
    dims = (((1,), (1,)), ((), ())) if transposed else (((1,), (0,)), ((), ()))
    x_high, x_low = split(x)
    t_high = table_ref[0, :, first : first + count]
    t_low = table_ref[1, :, first : first + count]
    dot = functools.partial(lax.dot_general, dimension_numbers=dims, preferred_element_type=F32)
    return dot(x_high, t_high) + (dot(x_low, t_high) + dot(x_high, t_low))


def spin(x, shift):
    shift = shift % 128
    return x if shift == 0 else pltpu.roll(x, shift, axis=1)


def filter_rows(x, table_ref, limit):
    vec = x[0].shape[0]
    c1, c2 = math.cos(2 * math.pi / 5), math.cos(4 * math.pi / 5)
    s1, s2 = math.sin(2 * math.pi / 5), math.sin(4 * math.pi / 5)
    sum1, dif1 = x[1] + x[4], x[1] - x[4]
    sum2, dif2 = x[2] + x[3], x[2] - x[3]
    z0 = x[0] + sum1 + sum2
    z1 = jnp.concatenate([x[0] + c1 * sum1 + c2 * sum2, s1 * dif1 + s2 * dif2], axis=0)
    z2 = jnp.concatenate([x[0] + c2 * sum1 + c1 * sum2, s2 * dif1 - s1 * dif2], axis=0)
    lane = lax.broadcasted_iota(jnp.int32, (vec, 128), 1)
    half = lane < 64
    slot = jnp.where(half, lane, lane - 64)
    sign = jnp.where(half, 1.0, -1.0).astype(F32)

    wave0 = 5 * slot
    weight0 = jnp.where(wave0 <= limit, jnp.where(wave0 == 0, 1.0 / LON, 2.0 / LON), 0.0)
    spec0 = dot3(z0, table_ref, 0, 128, False) * weight0
    back0 = dot3(spec0, table_ref, 0, 128, True)
    backs = []
    for z, first, low_wave, high_wave in ((z1, 128, 1, 4), (z2, 384, 2, 3)):
        wave = 5 * slot + jnp.where(half, low_wave, high_wave)
        weight = jnp.where(wave <= limit, 2.0 / LON, 0.0)
        flip = weight * sign
        y = dot3(z, table_ref, first, 256, False)
        cc, cs = y[:vec, :128], y[:vec, 128:]
        sc, ss = y[vec:, :128], y[vec:, 128:]
        a = cc - sign * ss
        b = cs + sign * sc
        even = jnp.concatenate([a * weight, b * weight], axis=1)
        odd = jnp.concatenate([b * flip, -(a * flip)], axis=1)
        back = dot3(jnp.concatenate([even, odd], axis=0), table_ref, first, 256, True)
        backs += [back[:vec], back[vec:]]
    e1, o1, e2, o2 = backs
    out = [back0 + e1 + e2]
    p, m = back0 + c1 * e1 + c2 * e2, s1 * o1 + s2 * o2
    r, n = back0 + c2 * e1 + c1 * e2, s2 * o1 - s1 * o2
    return out + [p + m, r + n, r - n, p - m]


def wrapped(last, first, lane):
    return jnp.where(lane < 64, last, jnp.where(lane < 96, spin(first, 64), spin(last, 64)))


def iotas():
    return (
        lax.broadcasted_iota(jnp.int32, (8, 128), 1),
        lax.broadcasted_iota(jnp.int32, (8, 128), 0),
    )


def load_kernel(
    band_ref, u_hbm, v_hbm, h_hbm, t_hbm, table_hbm, cutoff_hbm,
    u_ref, v_ref, h_ref, t_ref, last_ref, first_ref, table_ref, cutoff_ref, sems,
):
    pairs = (
        (u_hbm, u_ref), (v_hbm, v_ref), (cutoff_hbm, cutoff_ref), (table_hbm, table_ref),
        (h_hbm, h_ref), (t_hbm, t_ref),
    )
    copies = [pltpu.make_async_copy(src, dst, sems.at[n]) for n, (src, dst) in enumerate(pairs)]
    for copy in copies:
        copy.start()
    band = band_ref[0]
    bands = POLAR // ROWS
    own = jnp.logical_or(band < bands, band >= BANDS - bands)
    entry = jnp.where(band < bands, band, band - (BANDS - 2 * bands)) * ROWS
    for copy in copies[:4]:
        copy.wait()

    @pl.when(own)
    def _():
        row = lax.broadcasted_iota(jnp.int32, (8, 128), 0)
        limit = jnp.zeros((8, 128), jnp.int32)
        for r in range(ROWS):
            limit = jnp.where(row == r, cutoff_ref[entry + r], limit)
        spans = [slice(PART * q, PART * (q + 1)) for q in range(RADIX)]
        x = [
            jnp.concatenate([ref[:, :, at].reshape(32, PART) for ref in (u_ref, v_ref)], axis=0)
            for at in spans
        ]
        for at, piece in zip(spans, filter_rows(x, table_ref, jnp.concatenate([limit] * 8, axis=0))):
            u_ref[:, :, at] = piece[0:32].reshape(4, 8, PART)
            v_ref[:, :, at] = piece[32:64].reshape(4, 8, PART)

    for f, ref in enumerate((v_ref, h_ref, t_ref)):
        if f:
            copies[f + 3].wait()
        for l in range(LEV_DEV):
            last_ref[f, l : l + 1, :] = ref[l, ROWS - 1 : ROWS, :]
            first_ref[f, l : l + 1, :] = ref[l, 0:1, :]


def advance_kernel(u_ref, v_ref, h_ref, t_ref, part_ref, tail_ref):
    lane, row = iotas()
    fields = (u_ref, v_ref, h_ref, t_ref)
    for l in range(LEV_DEV):
        for f, ref in enumerate(fields):
            tail_ref[f, l, :, 0:64] = ref[l, :, LON - 64 : LON]
            tail_ref[f, l] = wrapped(tail_ref[f, l], ref[l, :, 0:128], lane)

    scale = COURANT * 0.25
    def level(l, _):

        def load(f, i):
            at = slice(128 * i, 128 * (i + 1))
            if i == CHUNKS - 1:
                return tail_ref[f, l]
            return fields[f][l, :, at]

        i = CHUNKS - 1
        u, h = load(0, i), load(2, i)
        q = h * load(3, i)
        before = tuple(spin(z, 1) for z in (u, h, q))
        flux = {}
        state = {}
        for i in range(CHUNKS + 1):
            if i < CHUNKS:
                u, v, h = load(0, i), load(1, i), load(2, i)
                q = h * load(3, i)
                now = tuple(spin(z, 1) for z in (u, h, q))
                ul, hl, ql = (jnp.where(lane == 0, b, n) for b, n in zip(before, now))
                before = now
                face = u + ul
                fh, fq = face * (h + hl), face * (q + ql)
                turned = (spin(fh, -1), spin(fq, -1))
                if i == 0:
                    first = turned
                vp, hp, qp = (pltpu.roll(z, 7, axis=0) for z in (v, h, q))
                wp = v + vp
                gh = jnp.where(row == 7, 0.0, wp * (h + hp))
                gq = jnp.where(row == 7, 0.0, wp * (q + qp))
                gh = gh - pltpu.roll(gh, 1, axis=0) - fh
                gq = gq - pltpu.roll(gq, 1, axis=0) - fq
                state[i] = (h, q, gh, gq)
                flux[i] = turned
            if i >= 1:
                k = i - 1
                nxt = flux[i] if i < CHUNKS else first
                h0, q0, gh0, gq0 = state.pop(k)
                mine = flux.pop(k)
                rh = jnp.where(lane == 127, nxt[0], mine[0])
                rq = jnp.where(lane == 127, nxt[1], mine[1])
                at = slice(128 * k, 128 * (k + 1))
                part_ref[0, l, :, at] = h0 - scale * (rh + gh0)
                part_ref[1, l, :, at] = q0 - scale * (rq + gq0)
        return 0

    lax.fori_loop(0, LEV_DEV, level, 0)


def pack_kernel(
    south_ref, north_ref, first_ref, last_ref, u_ref, part_ref,
    out_ref, halo_ref, edge_ref, flux_ref, n_ref,
):
    lane, row = iotas()
    end = slice(EXT - 128, EXT)
    for f in range(3):
        halo_ref[f, 0:4, 0:LON] = south_ref[f]
        halo_ref[f, 4:8, 0:LON] = north_ref[f]
        edge_ref[f, 0:4, 0:LON] = first_ref[f]
        edge_ref[f, 4:8, 0:LON] = last_ref[f]
        for ref in (halo_ref, edge_ref):
            ref[f, :, end] = wrapped(ref[f, :, end], ref[f, :, 0:128], lane)

    scale = COURANT * 0.25
    sign = jnp.where(row < 4, scale, -scale).astype(F32)
    for i in range(CHUNKS):
        at = slice(128 * i, 128 * (i + 1))
        v, h, t = (halo_ref[f, :, at] for f in range(3))
        w = (v + edge_ref[0, :, at]) * sign
        faces = w * (h + edge_ref[1, :, at]), w * (h * t + edge_ref[1, :, at] * edge_ref[2, :, at])
        for m, face in enumerate(faces):
            for r in range(8):
                flux_ref[m, r, :, at] = face[r : r + 1]

    def finish(l, _):
        for i in range(CHUNKS):
            at = slice(128 * i, 128 * (i + 1))

            def outer(m):
                low = jnp.broadcast_to(flux_ref[m, l, :, at], (8, 128))
                high = jnp.broadcast_to(flux_ref[m, l + 4, :, at], (8, 128))
                return jnp.where(row == 0, low, jnp.where(row == 7, high, 0.0))

            new_h = part_ref[0, l, :, at] + outer(0)
            new_q = part_ref[1, l, :, at] + outer(1)
            if i < CHUNKS - 1:
                n_ref[0, l, :, at] = u_ref[l, :, at]
            n_ref[1, l, :, at] = new_q / new_h
            n_ref[2, l, :, at] = new_h
        n_ref[0, l, :, LON - 64 : LON] = u_ref[l, :, LON - 64 : LON]
        n_ref[0, l, :, end] = wrapped(n_ref[0, l, :, end], u_ref[l, :, 0:128], lane)
        return 0

    lax.fori_loop(0, LEV_DEV, finish, 0)

    def place(f, pair, with_sides):
        def fetch(l, i):
            return n_ref[f, 2 * pair + l, :, 128 * i : 128 * (i + 1)]

        for j in range(PEERS):
            tails = []
            for l in range(2):
                start = PIECE * j
                i, off = start // 128, start % 128
                slab = spin(fetch(l, i), -off)
                if off:
                    slab = jnp.where(lane < 128 - off, slab, spin(fetch(l, i + 1), -off))
                out_ref[j, f * 4 + 2 * pair + l] = slab
                i, off = (start + 128) // 128, (start + 128) % 128
                tail = spin(fetch(l, i), 64 * l - off)
                if off > 64:
                    other = spin(fetch(l, i + 1), 64 * l - off)
                    tail = jnp.where(lane < 64 * l + 128 - off, tail, other)
                tails.append(tail)
            packed = jnp.where(lane < 64, tails[0], tails[1])
            if with_sides:
                at = (PIECE * j - 1) % LON
                i, off = at // 128, at % 128
                packed = jnp.where(
                    lane == 127,
                    spin(fetch(0, i), 127 - off),
                    jnp.where(lane == 63, spin(fetch(1, i), 63 - off), packed),
                )
            out_ref[j, 12 + f * 2 + pair] = packed
        return 0

    lax.fori_loop(0, 4, lambda n, _: place(n // 2, n % 2, False), 0)
    lax.fori_loop(0, 2, lambda n, _: place(2, n, True), 0)


EDGE, AU, BU, CU, FU, AT, BT, CT, FT = range(9)
BLOCK = 8
WINDOW = 10
UNROLL = 2
MARGIN = 1e-5


def remap_kernel(
    sigma_ref, inverse_ref, row_ref, r_ref, wind_hbm, temp_hbm,
    s_ref, d_ref, f_ref, m_ref, x_ref, bound_ref, scalar_ref, wind_ref, temp_ref, sems, bound_sem,
):
    lane, row = iotas()
    left = lane < 64
    even = jnp.logical_or(jnp.logical_and(left, lane != 63), lane == 127)
    zero = jnp.zeros((8, 128), F32)

    def turn(x):
        return pltpu.roll(x, 64, axis=1)

    def unpack(n, carry):
        ea, eb, fua, fub, fta, ftb = carry
        for s in range(2):
            for pair in range(2):
                packs = [r_ref[2 * n + s, 12 + 2 * f + pair] for f in range(3)]
                turns = [turn(p) for p in packs]
                for odd in range(2):
                    l = 2 * pair + odd
                    k = n * 8 + s * 4 + l
                    ua, ta, ha = (r_ref[2 * n + s, 4 * f + l] for f in range(3))
                    ub = turns[0] if odd else packs[0]
                    tb, hb = (
                        jnp.where(even, o, p) if odd else jnp.where(even, p, o)
                        for p, o in zip(packs[1:], turns[1:])
                    )
                    pa = ea + 0.5 * ha
                    pb = eb + 0.5 * hb
                    ra, rb = pltpu.roll(pa, 1, axis=1), pltpu.roll(pb, 1, axis=1)
                    la, lb = pltpu.roll(pa, 127, axis=1), pltpu.roll(pb, 127, axis=1)
                    wa = jnp.where(lane == 127, lb, la) - jnp.where(lane == 0, rb, ra)
                    wb = lb - jnp.where(lane == 0, ra, rb)
                    ua = ua - PRESSURE_COEF * wa
                    ub = ub - PRESSURE_COEF * wb
                    ub = jnp.where(left, ub, turn(ub))
                    s_ref[k, 0, EDGE], s_ref[k, 1, EDGE] = ea, eb
                    d_ref[k, 0], d_ref[k, 1] = ha, hb
                    s_ref[k, 0, FU], s_ref[k, 1, FU] = fua, fub
                    s_ref[k, 0, FT], s_ref[k, 1, FT] = fta, ftb
                    f_ref[0, k, 0], f_ref[0, k, 1] = ua, ub
                    f_ref[1, k, 0], f_ref[1, k, 1] = ta, tb
                    ea, eb = ea + ha, eb + hb
                    fua, fub = fua + ha * ua, fub + hb * ub
                    fta, ftb = fta + ha * ta, ftb + hb * tb
        return ea, eb, fua, fub, fta, ftb

    sums = lax.fori_loop(0, PEERS // 2, unpack, (zero,) * 6)
    surface = sums[:2]
    inverse = tuple(1.0 / s for s in surface)
    for k in range(WINDOW):
        s_ref[LEVELS + k, :, EDGE] = jnp.full((2, 8, 128), 1e30, F32)

    targets = jnp.broadcast_to(row_ref[...], (8, 128))

    def tally(n, counts):
        for j in range(8):
            xa, xb = (s_ref[n * 8 + j, part, EDGE] * inverse[part] for part in range(2))
            x_ref[0, 8 * j : 8 * j + 8, :] = jnp.maximum(xa, xb)
            x_ref[1, 8 * j : 8 * j + 8, :] = jnp.minimum(xa, xb)
        out = []
        for side, best, shift in ((0, jnp.maximum, -MARGIN), (1, jnp.minimum, MARGIN)):
            ref = x_ref.at[side]
            rows = [ref[pl.ds(r, 8, stride=8), :] for r in range(8)]
            while len(rows) > 1:
                rows = [best(p, q) for p, q in zip(rows[::2], rows[1::2])]
            reduce = jnp.max if side == 0 else jnp.min
            edge = reduce(rows[0], axis=1, keepdims=True)
            out.append(counts[side] + jnp.where(edge <= targets + shift, 1.0, 0.0))
        return tuple(out)

    counts = lax.fori_loop(0, LEVELS // 8, tally, (zero, zero))
    low, high = (jnp.sum(c, axis=0, keepdims=True) for c in counts)
    low = jnp.maximum(low - 1.0, 0.0)
    bound_ref[...] = jnp.where(row == 0, low, high).astype(jnp.int32)
    to_scalars = pltpu.make_async_copy(bound_ref, scalar_ref, bound_sem)
    to_scalars.start()

    def middle(m, k):
        return (7.0 / 12.0) * (f_ref[m, k - 1] + f_ref[m, k]) - (1.0 / 12.0) * (
            f_ref[m, k - 2] + f_ref[m, k + 1]
        )

    def layer(k, lower, upper):
        rd = 1.0 / d_ref[k]
        square = rd * rd
        for m, (pa, pb, pc) in enumerate(((AU, BU, CU), (AT, BT, CT))):
            a0, a1, f = lower[m], upper[m], f_ref[m, k]
            rise, rest = f - a0, a1 - f
            s_ref[k, :, pa] = a0
            s_ref[k, :, pb] = rd * (rise + (rise - rest))
            s_ref[k, :, pc] = square * (rest - rise)

    def layers(n, lower):
        for j in range(4):
            k = 1 + 4 * n + j
            upper = tuple(middle(m, k + 1) for m in range(2))
            layer(k, lower, upper)
            lower = upper
        return lower

    last = LEVELS - 1
    second = tuple(0.5 * (f_ref[m, 0] + f_ref[m, 1]) for m in range(2))
    layer(0, tuple(f_ref[m, 0] for m in range(2)), second)
    lower = lax.fori_loop(0, 15, layers, second)
    for k in range(61, LEVELS):
        if k < last - 1:
            upper = tuple(middle(m, k + 1) for m in range(2))
        elif k == last - 1:
            upper = tuple(0.5 * (f_ref[m, last - 1] + f_ref[m, last]) for m in range(2))
        else:
            upper = tuple(f_ref[m, last] for m in range(2))
        layer(k, lower, upper)
        lower = upper

    to_scalars.wait()

    def places(g):
        i = 2 * g
        s0, s1 = sigma_ref[i], sigma_ref[i + 1]
        return (
            (surface[0] * s0, 0),
            (surface[0] * s1, 0),
            (surface[1] * jnp.where(left, s0, s1), 1),
        )

    def begin(points, low):
        return tuple(tuple(s_ref[low, part, plane] for plane in range(9)) for _, part in points)

    def pick(points, k, state):
        values = [[s_ref[k, part, plane] for plane in range(9)] for part in range(2)]
        out = []
        for (p, part), held in zip(points, state):
            inside = p >= values[part][EDGE]
            out.append(tuple(jnp.where(inside, v, h) for v, h in zip(values[part], held)))
        return tuple(out)

    def mass_of(g, points, state):
        slots = (2 * g, 2 * g + 1, LEVELS + g)
        for slot, (p, _), held in zip(slots, points, state):
            y = p - held[EDGE]
            for m, (a, b, c, f) in enumerate(((AU, BU, CU, FU), (AT, BT, CT, FT))):
                m_ref[m, slot] = held[f] + y * (held[a] + y * (held[b] + y * held[c]))

    def pairs(n, _):
        for j in range(UNROLL):
            g = UNROLL * n + j
            points = places(g)
            low = scalar_ref[0, 2 * g]
            state = begin(points, low)
            for k in range(1, WINDOW):
                state = pick(points, low + k, state)
            mass_of(g, points, state)
        for j in range(UNROLL):
            g = UNROLL * n + j
            low, high = scalar_ref[0, 2 * g], scalar_ref[1, 2 * g + 1]

            @pl.when(high - low > WINDOW)
            def _():
                points = places(g)
                state = lax.fori_loop(
                    low + 1, high, functools.partial(pick, points), begin(points, low)
                )
                mass_of(g, points, state)

        return 0

    def leave(b, m):
        ref, hbm = ((wind_ref, wind_hbm), (temp_ref, temp_hbm))[m]
        at = pl.ds(b * BLOCK, BLOCK)
        return pltpu.make_async_copy(ref.at[at], hbm.at[at], sems.at[m, b])

    def block(b, carry):
        lax.fori_loop(b * (BLOCK // 2 // UNROLL), (b + 1) * (BLOCK // 2 // UNROLL), pairs, 0)
        carry = list(carry)
        for m, ref in enumerate((wind_ref, temp_ref)):
            for j in range(BLOCK // 2):
                i = b * BLOCK + 2 * j
                masses = m_ref[m, i], m_ref[m, i + 1]
                tail = m_ref[m, LEVELS + b * (BLOCK // 2) + j]
                turned = turn(tail)
                tails = tail, turned
                for n in range(2):
                    width = inverse_ref[i + n]
                    ref[i + n, :, 0:128] = (masses[n] - carry[2 * m]) * (inverse[0] * width)
                    value = (tails[n] - carry[2 * m + 1]) * (inverse[1] * width)
                    ref[i + n, :, 128:PIECE] = value[:, 0:TAIL]
                    carry[2 * m], carry[2 * m + 1] = masses[n], tails[n]
            leave(b, m).start()
        return tuple(carry)

    lax.fori_loop(0, LEVELS // BLOCK, block, (zero,) * 4)
    for b in range(LEVELS // BLOCK):
        for m in range(2):
            leave(b, m).wait()


VMEM = pltpu.MemorySpace.VMEM


def whole(space=pltpu.VMEM):
    return pl.BlockSpec(memory_space=space)


def keep(x):
    return pltpu.with_memory_space_constraint(x, VMEM)


def local(zonal_wind, merid_wind, thickness, potential_temp, cutoff, sigma_weights):
    band = lax.axis_index("lat").astype(jnp.int32).reshape(1)
    up = [(i, i + 1) for i in range(BANDS - 1)]
    down = [(i + 1, i) for i in range(BANDS - 1)]
    inputs = (zonal_wind, merid_wind, thickness, potential_temp)
    edge = pltpu.VMEM((3, LEV_DEV, LON), F32)
    field = pltpu.VMEM((LEV_DEV, ROWS, LON), F32)
    table = mode_table()
    *fields, last, first = pl.pallas_call(
        load_kernel,
        name="load",
        compiler_params=pltpu.CompilerParams(vmem_limit_bytes=16 << 20),
        out_shape=(field,) * 4 + (edge,) * 2,
        in_specs=[whole(pltpu.SMEM)] + [whole(pltpu.HBM)] * 6,
        out_specs=(whole(),) * 6,
        scratch_shapes=[
            pltpu.VMEM(table.shape, BF16),
            pltpu.SMEM(cutoff.shape, jnp.int32),
            pltpu.SemaphoreType.DMA((6,)),
        ],
    )(
        band,
        *(
            pltpu.with_memory_space_constraint(x, pltpu.HBM)
            for x in (*inputs, jnp.asarray(table), cutoff)
        ),
    )
    fields = [keep(x) for x in fields]
    south = lax.ppermute(last, "lat", up)
    north = lax.ppermute(first, "lat", down)
    (part,) = pl.pallas_call(
        advance_kernel,
        name="advance",
        compiler_params=pltpu.CompilerParams(vmem_limit_bytes=16 << 20),
        out_shape=(pltpu.VMEM((2, LEV_DEV, ROWS, EXT), F32),),
        in_specs=[whole()] * 4,
        out_specs=(whole(),),
        scratch_shapes=[pltpu.VMEM((4, LEV_DEV, ROWS, 128), F32)],
    )(*fields)
    outgoing = pl.pallas_call(
        pack_kernel,
        name="pack",
        compiler_params=pltpu.CompilerParams(vmem_limit_bytes=16 << 20),
        out_shape=pltpu.VMEM((PEERS, 18, 8, 128), F32),
        in_specs=[whole()] * 6,
        out_specs=whole(),
        scratch_shapes=[
            pltpu.VMEM((3, 8, EXT), F32),
            pltpu.VMEM((3, 8, EXT), F32),
            pltpu.VMEM((2, 8, 1, EXT), F32),
            pltpu.VMEM((3, LEV_DEV, ROWS, EXT), F32),
        ],
    )(*map(keep, (south, north, first, last)), fields[0], keep(part))
    columns = lax.all_to_all(outgoing, "lev", split_axis=0, concat_axis=0, tiled=True)
    total = jnp.sum(sigma_weights)
    sigma = jnp.cumsum(sigma_weights) / total
    inverse = total / sigma_weights
    sigma_row = jnp.pad(sigma, (0, 128 - LEVELS), constant_values=2.0).reshape(1, 128)
    shape = jax.ShapeDtypeStruct((LEVELS, ROWS, PIECE), F32)
    return pl.pallas_call(
        remap_kernel,
        name="remap",
        compiler_params=pltpu.CompilerParams(vmem_limit_bytes=24 << 20),
        out_shape=(shape, shape),
        in_specs=[whole(pltpu.SMEM)] * 2 + [whole()] * 2,
        out_specs=(whole(pltpu.HBM), whole(pltpu.HBM)),
        scratch_shapes=[
            pltpu.VMEM((LEVELS + WINDOW, 2, 9, 8, 128), F32),
            pltpu.VMEM((LEVELS, 2, 8, 128), F32),
            pltpu.VMEM((2, LEVELS, 2, 8, 128), F32),
            pltpu.VMEM((2, LEVELS + LEVELS // 2, 8, 128), F32),
            pltpu.VMEM((2, 64, 128), F32),
            pltpu.VMEM((8, 128), jnp.int32),
            pltpu.SMEM((8, 128), jnp.int32),
            pltpu.VMEM((LEVELS, ROWS, PIECE), F32),
            pltpu.VMEM((LEVELS, ROWS, PIECE), F32),
            pltpu.SemaphoreType.DMA((2, LEVELS // BLOCK)),
            pltpu.SemaphoreType.DMA,
        ],
    )(sigma, inverse, sigma_row, keep(columns))


def solution(mesh):
    field = P("lev", "lat", None)
    out = P(None, "lat", "lev")
    return jax.shard_map(
        local,
        mesh=mesh,
        in_specs=(field, field, field, field, P(), P()),
        out_specs=(out, out),
        check_vma=False,
    )
```

time: 284 us -> 50.8 us (0.18)
  the two profiles are of different devices: /device:TPU:32 before, /device:TPU:128 now
where the time goes in v2:
time: 50.8 us; the launch traced here: 50.5 us
  waiting for transfers between devices  20.2 us (40%)
  starting transfers between devices  13.9 us (27%)
  Pallas kernels  13.5 us (27%)
  other arithmetic  2.1 us (4%)
  between operations  0.71 us (1%)
    all_to_all x1, waiting for transfers between devices, local(): lax.all_to_all(outgoing, 'lev', split_axis=0, concat_axis=0, tiled=True)  18.8 us
    pallas_call x1, Pallas kernels, local(): pl.pallas_call(remap_kernel, name='remap', compiler_params=pltpu.Compiler...  7.77 us
    all_to_all x1, starting transfers between devices, local(): lax.all_to_all(outgoing, 'lev', split_axis=0, concat_axis=0, tiled=True)  7.17 us
    ppermute x1, starting transfers between devices, local(): north = lax.ppermute(first, 'lat', down)  4.85 us
    pallas_call x1, Pallas kernels, local(): pl.pallas_call(pack_kernel, name='pack', compiler_params=pltpu.CompilerPa...  2.66 us
    ppermute x1, starting transfers between devices, local(): south = lax.ppermute(last, 'lat', up)  1.92 us
    pallas_call x1, Pallas kernels, local(): pl.pallas_call(load_kernel, name='load', compiler_params=pltpu.CompilerPa...  1.85 us
    ppermute x1, waiting for transfers between devices, local(): north = lax.ppermute(first, 'lat', down)  1.36 us
  transfers between devices with their start and end apart: 3, of which 2 were waited for; matrix products, arithmetic and copies ran while one was open for 4% of the time, Pallas kernels for 2%

profile of v2, /device:TPU:128, one launch (start us, length us, event | category | flops | bytes accessed | tf_op | source)
XLA Modules:
  0.0 50.5 jit_solution(17749740282528003565)
XLA Ops:
  0.6 1.9 %load.1 = (f32[4,8,2880]{2,1,0:T(8,128)S(1)}, f32[4,8,2880]{2,1,0:T(8,128)S(1)}, f32[4,8,2880]{2,1,0:T(8,128)S(1)}, f32[4,8,2880]{2,1,0:T(8,128)S(1)}, f32[3,4,2...) custom-call(s32[1]{0:T(128)} %bitcast.2.band_ref, f32[4,8,2880]{2,1,0:T(8,128)} %u_hbm.1, f32[4,8,2880]{2,1,0:T(8,128)} %v_hbm.1, ...), custom_call_target="tpu_custom_call" | custom-call | tf_op jit(solution)/shard_map/load/pallas_call | solution.py:520
  2.5 1.9 %collective-permute-start = (f32[3,4,2880]{2,1,0:T(4,128)S(1)}, f32[3,4,2880]{2,1,0:T(4,128)S(1)}, u32[]{:S(2)}, u32[]{:S(2)}) collective-permute-start(f32[3,4,2880]{2,1,0:T(4,128)S(1)} %get-tuple-element.8.last_ref), channel_id=1, source_target_pairs={{0,16},{16,32},{32,48},{48,64},{64,80},{80,96},{96,112},{112,128},... | collective-permute-start | bytes 414728 | tf_op jit(solution)/shard_map/ppermute | solution.py:540
  4.4 4.9 %collective-permute-start.1 = (f32[3,4,2880]{2,1,0:T(4,128)S(1)}, f32[3,4,2880]{2,1,0:T(4,128)S(1)}, u32[]{:S(2)}, u32[]{:S(2)}) collective-permute-start(f32[3,4,2880]{2,1,0:T(4,128)S(1)} %get-tuple-element.9.first_ref), channel_id=1, source_target_pairs={{16,0},{32,16},{48,32},{64,48},{80,64},{96,80},{112,96},{128,112},... | collective-permute-start | bytes 414728 | tf_op jit(solution)/shard_map/ppermute | solution.py:541
  9.3 1.2 %advance.1.part_ref = f32[2,4,8,2944]{3,2,1,0:T(8,128)S(1)} custom-call(f32[4,8,2880]{2,1,0:T(8,128)S(1)} %get-tuple-element.10.u_ref, f32[4,8,2880]{2,1,0:T(8,128)S(1)} %get-tuple-element.11.v_ref, f32[4,8,2880]{2,1,0:T(8,128)S(1)} %get-tuple-element.12.h_ref, f32[4,8,2880]{2,1,0:T(8,128)S(1)} %get-tuple-element.13.t_ref), custom_call_target="tpu_custom_call" | custom-call | tf_op jit(solution)/shard_map/advance/pallas_call | solution.py:542
  10.5 0.0 collective-permute-done.south_ref
  10.5 1.4 %collective-permute-done.1.north_ref = f32[3,4,2880]{2,1,0:T(4,128)S(1)} collective-permute-done((f32[3,4,2880]{2,1,0:T(4,128)S(1)}, f32[3,4,2880]{2,1,0:T(4,128)S(1)}, u32[]{:S(2)}, u32[]{:S(2)}) %collective-permute-start.1) | collective-permute-done | bytes 138272 | tf_op jit(solution)/shard_map/ppermute | solution.py:541
  11.9 2.7 %pack.1 = f32[16,18,8,128]{3,2,1,0:T(8,128)} custom-call(f32[3,4,2880]{2,1,0:T(4,128)S(1)} %collective-permute-done.south_ref, f32[3,4,2880]{2,1,0:T(4,128)S(1)} %collective-permute-done.1.north_ref, f32[3,4,2880]{2,1,0:T(4,128)S(1)} %get-tuple-element.9.first_ref, f32[3,4,2880]{2,1,0:T(4,128)S(1)} %get-tuple-element.8.last_ref, ...), custom_call_target="tpu_custom_call" | custom-call | tf_op jit(solution)/shard_map/pack/pallas_call | solution.py:551
  14.5 0.0 copy-start
  14.5 7.2 %all-to-all-start = ((f32[16,18,8,128]{3,2,1,0:T(8,128)}), f32[16,18,8,128]{3,2,1,0:T(8,128)S(1)}, u32[]{:S(2)}, u32[]{:S(2)}) async-start(f32[16,18,8,128]{3,2,1,0:T(8,128)} %pack.1), calls=%async_computation | async-start | bytes 2359296 | tf_op jit(solution)/shard_map/all_to_all | solution.py:565
  21.7 0.0 copy-done
  21.7 0.6 %reduce_sum.9 = f32[]{:T(128)} reduce(f32[64]{0:T(128)S(1)} %copy-done, f32[]{:T(128)} %constant.5.clone.1), dimensions={0}, to_apply=%region_1.0 | reduce | flops 63 | bytes 264 | tf_op jit(solution)/shard_map/reduce_sum | solution.py:566
  22.3 0.1 copy.10
  22.4 0.1 reduce-window.9
  22.5 0.8 %divide_reduce_fusion.sigma_ref = f32[64]{0:T(128)S(1)} fusion(f32[64,1]{1,0:T(8,128)S(1)} %reduce-window.9, f32[]{:T(128)} %reduce_sum.9), kind=kLoop, calls=%fused_computation | loop fusion | flops 64 | bytes 516 | tf_op jit(solution)/shard_map/div | solution.py:567
  23.3 0.7 %broadcast_divide_fusion.inverse_ref = f32[64]{0:T(128)S(1)} fusion(f32[64]{0:T(128)S(1)} %copy-done, f32[]{:T(128)} %reduce_sum.9), kind=kLoop, calls=%fused_computation.2 | loop fusion | flops 64 | bytes 516 | tf_op jit(solution)/shard_map/div | solution.py:568
  23.9 18.8 %all-to-all-done.r_ref = f32[16,18,8,128]{3,2,1,0:T(8,128)S(1)} async-done(((f32[16,18,8,128]{3,2,1,0:T(8,128)}), f32[16,18,8,128]{3,2,1,0:T(8,128)S(1)}, u32[]{:S(2)}, u32[]{:S(2)}) %all-to-all-start) | async-done | bytes 1179680 | tf_op jit(solution)/shard_map/all_to_all | solution.py:565
  42.8 7.8 %remap.1 = (f32[64,8,180]{2,1,0:T(8,128)}, f32[64,8,180]{2,1,0:T(8,128)}) custom-call(f32[64]{0:T(128)S(1)} %divide_reduce_fusion.sigma_ref, f32[64]{0:T(128)S(1)} %broadcast_divide_fusion.inverse_ref, f32[1,128]{1,0:T(1,128)S(1)} %pad_bitcast_fusion.row_ref, f32[16,18,8,128]{3,2,1,0:T(8,128)S(1)} %all-to-all-done.r_ref), custom_call_target="tpu_custom_call" | custom-call | tf_op jit(solution)/shard_map/remap/pallas_call | solution.py:571
  (1 shorter events, 0.0 us)
Async XLA Ops:
  2.5 8.0 %collective-permute-start = (f32[3,4,2880]{2,1,0:T(4,128)S(1)}, f32[3,4,2880]{2,1,0:T(4,128)S(1)}, u32[]{:S(2)}, u32[]{:S(2)}) collective-permute-start(f32[3,4,2880]{2,1,0:T(4,128)S(1)} %get-tuple-element.8.last_ref), channel_id=1, source_target_pairs={{0,16},{16,32},{32,48},{48,64},{64,80},{80,96},{96,112},{112,128},... | collective-permute-start | bytes 414728 | tf_op jit(solution)/shard_map/ppermute | solution.py:540
  4.4 7.5 %collective-permute-start.1 = (f32[3,4,2880]{2,1,0:T(4,128)S(1)}, f32[3,4,2880]{2,1,0:T(4,128)S(1)}, u32[]{:S(2)}, u32[]{:S(2)}) collective-permute-start(f32[3,4,2880]{2,1,0:T(4,128)S(1)} %get-tuple-element.9.first_ref), channel_id=1, source_target_pairs={{16,0},{32,16},{48,32},{64,48},{80,64},{96,80},{112,96},{128,112},... | collective-permute-start | bytes 414728 | tf_op jit(solution)/shard_map/ppermute | solution.py:541
  14.5 7.2 %copy-start = (f32[64]{0:T(128)S(1)}, f32[64]{0:T(128)}, u32[]{:S(2)}) copy-start(f32[64]{0:T(128)} %param.12) | copy-start | bytes 772
  14.5 28.2 %all-to-all-start = ((f32[16,18,8,128]{3,2,1,0:T(8,128)}), f32[16,18,8,128]{3,2,1,0:T(8,128)S(1)}, u32[]{:S(2)}, u32[]{:S(2)}) async-start(f32[16,18,8,128]{3,2,1,0:T(8,128)} %pack.1), calls=%async_computation | async-start | bytes 2359296 | tf_op jit(solution)/shard_map/all_to_all | solution.py:565

commit v3 on v2

--- a/solution.py
+++ b/solution.py
@@ -155,13 +155,58 @@
             first_ref[f, l : l + 1, :] = ref[l, 0:1, :]
 
 
-def advance_kernel(u_ref, v_ref, h_ref, t_ref, part_ref, tail_ref):
+def place(slot_ref, fetch, lane, with_sides):
+    for j in range(PEERS):
+        tails = []
+        for l in range(2):
+            start = PIECE * j
+            i, off = start // 128, start % 128
+            slab = spin(fetch(l, i), -off)
+            if off:
+                slab = jnp.where(lane < 128 - off, slab, spin(fetch(l, i + 1), -off))
+            slot_ref[j, l] = slab
+            i, off = (start + 128) // 128, (start + 128) % 128
+            tail = spin(fetch(l, i), 64 * l - off)
+            if off > 64:
+                other = spin(fetch(l, i + 1), 64 * l - off)
+                tail = jnp.where(lane < 64 * l + 128 - off, tail, other)
+            tails.append(tail)
+        packed = jnp.where(lane < 64, tails[0], tails[1])
+        if with_sides:
+            at = (PIECE * j - 1) % LON
+            i, off = at // 128, at % 128
+            packed = jnp.where(
+                lane == 127,
+                spin(fetch(0, i), 127 - off),
+                jnp.where(lane == 63, spin(fetch(1, i), 63 - off), packed),
+            )
+        slot_ref[j, 2] = packed
+
+
+def send(slots_ref, out_hbm, sems, slot, group):
+    dst = out_hbm.at[:, pl.ds(group, 3)]
+    return pltpu.make_async_copy(slots_ref.at[slot], dst, sems.at[slot])
+
+
+def advance_kernel(u_ref, v_ref, h_ref, t_ref, part_ref, out_hbm, tail_ref, slots_ref, sems):
     lane, row = iotas()
     fields = (u_ref, v_ref, h_ref, t_ref)
     for l in range(LEV_DEV):
         for f, ref in enumerate(fields):
             tail_ref[f, l, :, 0:64] = ref[l, :, LON - 64 : LON]
             tail_ref[f, l] = wrapped(tail_ref[f, l], ref[l, :, 0:128], lane)
+
+    def put(pair, _):
+        def fetch(l, i):
+            if i == CHUNKS - 1:
+                return tail_ref[0, 2 * pair + l]
+            return u_ref[2 * pair + l, :, 128 * i : 128 * (i + 1)]
+
+        place(slots_ref.at[pair], fetch, lane, False)
+        send(slots_ref, out_hbm, sems, pair, 3 * pair).start()
+        return 0
+
+    lax.fori_loop(0, 2, put, 0)
 
     scale = COURANT * 0.25
     def level(l, _):
@@ -211,11 +256,13 @@
         return 0
 
     lax.fori_loop(0, LEV_DEV, level, 0)
+    for pair in range(2):
+        send(slots_ref, out_hbm, sems, pair, 3 * pair).wait()
 
 
 def pack_kernel(
-    south_ref, north_ref, first_ref, last_ref, u_ref, part_ref,
-    out_ref, halo_ref, edge_ref, flux_ref, n_ref,
+    south_ref, north_ref, first_ref, last_ref, part_ref, wind_hbm,
+    out_hbm, halo_ref, edge_ref, flux_ref, n_ref, slots_ref, sems,
 ):
     lane, row = iotas()
     end = slice(EXT - 128, EXT)
@@ -249,49 +296,26 @@
 
             new_h = part_ref[0, l, :, at] + outer(0)
             new_q = part_ref[1, l, :, at] + outer(1)
-            if i < CHUNKS - 1:
-                n_ref[0, l, :, at] = u_ref[l, :, at]
-            n_ref[1, l, :, at] = new_q / new_h
-            n_ref[2, l, :, at] = new_h
-        n_ref[0, l, :, LON - 64 : LON] = u_ref[l, :, LON - 64 : LON]
-        n_ref[0, l, :, end] = wrapped(n_ref[0, l, :, end], u_ref[l, :, 0:128], lane)
+            n_ref[0, l, :, at] = new_q / new_h
+            n_ref[1, l, :, at] = new_h
         return 0
 
     lax.fori_loop(0, LEV_DEV, finish, 0)
 
-    def place(f, pair, with_sides):
+    def put(pair, f):
         def fetch(l, i):
-            return n_ref[f, 2 * pair + l, :, 128 * i : 128 * (i + 1)]
-
-        for j in range(PEERS):
-            tails = []
-            for l in range(2):
-                start = PIECE * j
-                i, off = start // 128, start % 128
-                slab = spin(fetch(l, i), -off)
-                if off:
-                    slab = jnp.where(lane < 128 - off, slab, spin(fetch(l, i + 1), -off))
-                out_ref[j, f * 4 + 2 * pair + l] = slab
-                i, off = (start + 128) // 128, (start + 128) % 128
-                tail = spin(fetch(l, i), 64 * l - off)
-                if off > 64:
-                    other = spin(fetch(l, i + 1), 64 * l - off)
-                    tail = jnp.where(lane < 64 * l + 128 - off, tail, other)
-                tails.append(tail)
-            packed = jnp.where(lane < 64, tails[0], tails[1])
-            if with_sides:
-                at = (PIECE * j - 1) % LON
-                i, off = at // 128, at % 128
-                packed = jnp.where(
-                    lane == 127,
-                    spin(fetch(0, i), 127 - off),
-                    jnp.where(lane == 63, spin(fetch(1, i), 63 - off), packed),
-                )
-            out_ref[j, 12 + f * 2 + pair] = packed
+            return n_ref[f - 1, 2 * pair + l, :, 128 * i : 128 * (i + 1)]
+
+        slot = 2 * (f - 1) + pair
+        place(slots_ref.at[slot], fetch, lane, f == 2)
+        send(slots_ref, out_hbm, sems, slot, 6 * f + 3 * pair).start()
         return 0
 
-    lax.fori_loop(0, 4, lambda n, _: place(n // 2, n % 2, False), 0)
-    lax.fori_loop(0, 2, lambda n, _: place(2, n, True), 0)
+    for f in (1, 2):
+        lax.fori_loop(0, 2, lambda pair, _, f=f: put(pair, f), 0)
+    for f in (1, 2):
+        for pair in range(2):
+            send(slots_ref, out_hbm, sems, 2 * (f - 1) + pair, 6 * f + 3 * pair).wait()
 
 
 EDGE, AU, BU, CU, FU, AT, BT, CT, FT = range(9)
@@ -303,7 +327,7 @@
 
 def remap_kernel(
     sigma_ref, inverse_ref, row_ref, r_ref, wind_hbm, temp_hbm,
-    s_ref, d_ref, f_ref, m_ref, x_ref, bound_ref, scalar_ref, wind_ref, temp_ref, sems, bound_sem,
+    s_ref, d_ref, f_ref, m_ref, x_ref, y_ref, bound_ref, scalar_ref, wind_ref, temp_ref, sems, bound_sem,
 ):
     lane, row = iotas()
     left = lane < 64
@@ -317,12 +341,12 @@
         ea, eb, fua, fub, fta, ftb = carry
         for s in range(2):
             for pair in range(2):
-                packs = [r_ref[2 * n + s, 12 + 2 * f + pair] for f in range(3)]
+                packs = [r_ref[2 * n + s, 6 * f + 3 * pair + 2] for f in range(3)]
                 turns = [turn(p) for p in packs]
                 for odd in range(2):
                     l = 2 * pair + odd
                     k = n * 8 + s * 4 + l
-                    ua, ta, ha = (r_ref[2 * n + s, 4 * f + l] for f in range(3))
+                    ua, ta, ha = (r_ref[2 * n + s, 6 * f + 3 * pair + odd] for f in range(3))
                     ub = turns[0] if odd else packs[0]
                     tb, hb = (
                         jnp.where(even, o, p) if odd else jnp.where(even, p, o)
@@ -356,23 +380,24 @@
 
     targets = jnp.broadcast_to(row_ref[...], (8, 128))
 
-    def tally(n, counts):
+    def tally(n, _):
         for j in range(8):
             xa, xb = (s_ref[n * 8 + j, part, EDGE] * inverse[part] for part in range(2))
             x_ref[0, 8 * j : 8 * j + 8, :] = jnp.maximum(xa, xb)
             x_ref[1, 8 * j : 8 * j + 8, :] = jnp.minimum(xa, xb)
-        out = []
-        for side, best, shift in ((0, jnp.maximum, -MARGIN), (1, jnp.minimum, MARGIN)):
+        for side, best in ((0, jnp.maximum), (1, jnp.minimum)):
             ref = x_ref.at[side]
             rows = [ref[pl.ds(r, 8, stride=8), :] for r in range(8)]
             while len(rows) > 1:
                 rows = [best(p, q) for p, q in zip(rows[::2], rows[1::2])]
-            reduce = jnp.max if side == 0 else jnp.min
-            edge = reduce(rows[0], axis=1, keepdims=True)
-            out.append(counts[side] + jnp.where(edge <= targets + shift, 1.0, 0.0))
-        return tuple(out)
-
-    counts = lax.fori_loop(0, LEVELS // 8, tally, (zero, zero))
+            y_ref[side, n] = rows[0]
+        return 0
+
+    lax.fori_loop(0, LEVELS // 8, tally, 0)
+    counts = []
+    for side, reduce, shift in ((0, jnp.max, -MARGIN), (1, jnp.min, MARGIN)):
+        ends = [reduce(y_ref[side, n], axis=1, keepdims=True) for n in range(LEVELS // 8)]
+        counts.append(sum(jnp.where(e <= targets + shift, 1.0, 0.0) for e in ends))
     low, high = (jnp.sum(c, axis=0, keepdims=True) for c in counts)
     low = jnp.maximum(low - 1.0, 0.0)
     bound_ref[...] = jnp.where(row == 0, low, high).astype(jnp.int32)
@@ -539,29 +564,38 @@
     fields = [keep(x) for x in fields]
     south = lax.ppermute(last, "lat", up)
     north = lax.ppermute(first, "lat", down)
-    (part,) = pl.pallas_call(
+    window = jax.ShapeDtypeStruct((PEERS, 18, 8, 128), F32)
+    slot = (PEERS, 3, 8, 128)
+    part, winds = pl.pallas_call(
         advance_kernel,
         name="advance",
         compiler_params=pltpu.CompilerParams(vmem_limit_bytes=16 << 20),
-        out_shape=(pltpu.VMEM((2, LEV_DEV, ROWS, EXT), F32),),
+        out_shape=(pltpu.VMEM((2, LEV_DEV, ROWS, EXT), F32), window),
         in_specs=[whole()] * 4,
-        out_specs=(whole(),),
-        scratch_shapes=[pltpu.VMEM((4, LEV_DEV, ROWS, 128), F32)],
+        out_specs=(whole(), whole(pltpu.HBM)),
+        scratch_shapes=[
+            pltpu.VMEM((4, LEV_DEV, ROWS, 128), F32),
+            pltpu.VMEM((2, *slot), F32),
+            pltpu.SemaphoreType.DMA((2,)),
+        ],
     )(*fields)
     outgoing = pl.pallas_call(
         pack_kernel,
         name="pack",
         compiler_params=pltpu.CompilerParams(vmem_limit_bytes=16 << 20),
-        out_shape=pltpu.VMEM((PEERS, 18, 8, 128), F32),
-        in_specs=[whole()] * 6,
-        out_specs=whole(),
+        out_shape=window,
+        input_output_aliases={5: 0},
+        in_specs=[whole()] * 5 + [whole(pltpu.HBM)],
+        out_specs=whole(pltpu.HBM),
         scratch_shapes=[
             pltpu.VMEM((3, 8, EXT), F32),
             pltpu.VMEM((3, 8, EXT), F32),
             pltpu.VMEM((2, 8, 1, EXT), F32),
-            pltpu.VMEM((3, LEV_DEV, ROWS, EXT), F32),
+            pltpu.VMEM((2, LEV_DEV, ROWS, EXT), F32),
+            pltpu.VMEM((4, *slot), F32),
+            pltpu.SemaphoreType.DMA((4,)),
         ],
-    )(*map(keep, (south, north, first, last)), fields[0], keep(part))
+    )(*map(keep, (south, north, first, last, part)), winds)
     columns = lax.all_to_all(outgoing, "lev", split_axis=0, concat_axis=0, tiled=True)
     total = jnp.sum(sigma_weights)
     sigma = jnp.cumsum(sigma_weights) / total
@@ -581,6 +615,7 @@
             pltpu.VMEM((2, LEVELS, 2, 8, 128), F32),
             pltpu.VMEM((2, LEVELS + LEVELS // 2, 8, 128), F32),
             pltpu.VMEM((2, 64, 128), F32),
+            pltpu.VMEM((2, LEVELS // 8, 8, 128), F32),
             pltpu.VMEM((8, 128), jnp.int32),
             pltpu.SMEM((8, 128), jnp.int32),
             pltpu.VMEM((LEVELS, ROWS, PIECE), F32),

time: 50.8 us -> 49 us (0.965)
  Pallas kernels: 13.5 us -> 12.3 us
    pallas_call x1, Pallas kernels: 7.77 us -> 6.99 us  [local(): pl.pallas_call(remap_kernel, name='remap', compiler_params=pltpu.Compiler...]
    pallas_call x1, Pallas kernels: 2.66 us -> 1.89 us  [local(): pl.pallas_call(pack_kernel, name='pack', compiler_params=pltpu.CompilerPa...]
  transfers between devices with their start and end apart: 3 -> 3, of which waited for: 2 -> 2; matrix products, arithmetic and copies ran while one was open for 4% -> 4% of each run, Pallas kernels for 2% -> 3%
where the time goes in v3:
time: 49 us; the launch traced here: 48.9 us
  waiting for transfers between devices  19.8 us (40%)
  starting transfers between devices  13.8 us (28%)
  Pallas kernels  12.3 us (25%)
  other arithmetic  2.1 us (4%)
  between operations  0.73 us (1%)
    all_to_all x1, waiting for transfers between devices, local(): lax.all_to_all(outgoing, 'lev', split_axis=0, concat_axis=0, tiled=True)  18.8 us
    all_to_all x1, starting transfers between devices, local(): lax.all_to_all(outgoing, 'lev', split_axis=0, concat_axis=0, tiled=True)  7.05 us
    pallas_call x1, Pallas kernels, local(): pl.pallas_call(remap_kernel, name='remap', compiler_params=pltpu.Compiler...  6.99 us
    ppermute x1, starting transfers between devices, local(): north = lax.ppermute(first, 'lat', down)  4.85 us
    ppermute x1, starting transfers between devices, local(): south = lax.ppermute(last, 'lat', up)  1.92 us
    pallas_call x1, Pallas kernels, local(): pl.pallas_call(pack_kernel, name='pack', compiler_params=pltpu.CompilerPa...  1.89 us
    pallas_call x1, Pallas kernels, local(): pl.pallas_call(load_kernel, name='load', compiler_params=pltpu.CompilerPa...  1.85 us
    pallas_call x1, Pallas kernels, local(): pl.pallas_call(advance_kernel, name='advance', compiler_params=pltpu.Comp...  1.59 us
  transfers between devices with their start and end apart: 3, of which 2 were waited for; matrix products, arithmetic and copies ran while one was open for 4% of the time, Pallas kernels for 3%

profile of v3, /device:TPU:128, one launch (start us, length us, event | category | flops | bytes accessed | tf_op | source)
XLA Modules:
  0.0 48.9 jit_solution(489484888118662127)
XLA Ops:
  0.6 1.9 %load.1 = (f32[4,8,2880]{2,1,0:T(8,128)S(1)}, f32[4,8,2880]{2,1,0:T(8,128)S(1)}, f32[4,8,2880]{2,1,0:T(8,128)S(1)}, f32[4,8,2880]{2,1,0:T(8,128)S(1)}, f32[3,4,2...) custom-call(s32[1]{0:T(128)} %bitcast.2.band_ref, f32[4,8,2880]{2,1,0:T(8,128)} %u_hbm.1, f32[4,8,2880]{2,1,0:T(8,128)} %v_hbm.1, ...), custom_call_target="tpu_custom_call" | custom-call | tf_op jit(solution)/shard_map/load/pallas_call | solution.py:545
  2.5 1.9 %collective-permute-start = (f32[3,4,2880]{2,1,0:T(4,128)S(1)}, f32[3,4,2880]{2,1,0:T(4,128)S(1)}, u32[]{:S(2)}, u32[]{:S(2)}) collective-permute-start(f32[3,4,2880]{2,1,0:T(4,128)S(1)} %get-tuple-element.10.last_ref), channel_id=1, source_target_pairs={{0,16},{16,32},{32,48},{48,64},{64,80},{80,96},{96,112},{112,128},... | collective-permute-start | bytes 414728 | tf_op jit(solution)/shard_map/ppermute | solution.py:565
  4.4 4.9 %collective-permute-start.1 = (f32[3,4,2880]{2,1,0:T(4,128)S(1)}, f32[3,4,2880]{2,1,0:T(4,128)S(1)}, u32[]{:S(2)}, u32[]{:S(2)}) collective-permute-start(f32[3,4,2880]{2,1,0:T(4,128)S(1)} %get-tuple-element.11.first_ref), channel_id=1, source_target_pairs={{16,0},{32,16},{48,32},{64,48},{80,64},{96,80},{112,96},{128,112},... | collective-permute-start | bytes 414728 | tf_op jit(solution)/shard_map/ppermute | solution.py:566
  9.3 1.6 %advance.1 = (f32[2,4,8,2944]{3,2,1,0:T(8,128)S(1)}, f32[16,18,8,128]{3,2,1,0:T(8,128)}) custom-call(f32[4,8,2880]{2,1,0:T(8,128)S(1)} %get-tuple-element.12.u_ref, f32[4,8,2880]{2,1,0:T(8,128)S(1)} %get-tuple-element.13.v_ref, f32[4,8,2880]{2,1,0:T(8,128)S(1)} %get-tuple-element.14.h_ref, f32[4,8,2880]{2,1,0:T(8,128)S(1)} %get-tuple-element.15.t_ref), custom_call_target="tpu_custom_call" | custom-call | tf_op jit(solution)/shard_map/advance/pallas_call | solution.py:569
  10.9 0.0 collective-permute-done.south_ref
  10.9 1.0 %collective-permute-done.1.north_ref = f32[3,4,2880]{2,1,0:T(4,128)S(1)} collective-permute-done((f32[3,4,2880]{2,1,0:T(4,128)S(1)}, f32[3,4,2880]{2,1,0:T(4,128)S(1)}, u32[]{:S(2)}, u32[]{:S(2)}) %collective-permute-start.1) | collective-permute-done | bytes 138272 | tf_op jit(solution)/shard_map/ppermute | solution.py:566
  11.9 1.9 %pack.1 = f32[16,18,8,128]{3,2,1,0:T(8,128)} custom-call(f32[3,4,2880]{2,1,0:T(4,128)S(1)} %collective-permute-done.south_ref, f32[3,4,2880]{2,1,0:T(4,128)S(1)} %collective-permute-done.1.north_ref, f32[3,4,2880]{2,1,0:T(4,128)S(1)} %get-tuple-element.11.first_ref, f32[3,4,2880]{2,1,0:T(4,128)S(1)} %get-tuple-element.10.last_ref, ...), custom_call_target="tpu_custom_call", output_to_operand_aliasing={{}: (5, {})} | custom-call | tf_op jit(solution)/shard_map/pack/pallas_call | solution.py:582
  13.8 0.0 copy-start
  13.8 7.0 %all-to-all-start = ((f32[16,18,8,128]{3,2,1,0:T(8,128)}), f32[16,18,8,128]{3,2,1,0:T(8,128)S(1)}, u32[]{:S(2)}, u32[]{:S(2)}) async-start(f32[16,18,8,128]{3,2,1,0:T(8,128)} %pack.1), calls=%async_computation | async-start | bytes 2359296 | tf_op jit(solution)/shard_map/all_to_all | solution.py:599
  20.8 0.0 copy-done
  20.8 0.6 %reduce_sum.9 = f32[]{:T(128)} reduce(f32[64]{0:T(128)S(1)} %copy-done, f32[]{:T(128)} %constant.5.clone.1), dimensions={0}, to_apply=%region_1.0 | reduce | flops 63 | bytes 264 | tf_op jit(solution)/shard_map/reduce_sum | solution.py:600
  21.5 0.1 copy.11
  21.5 0.1 reduce-window.9
  21.6 0.8 %divide_reduce_fusion.sigma_ref = f32[64]{0:T(128)S(1)} fusion(f32[64,1]{1,0:T(8,128)S(1)} %reduce-window.9, f32[]{:T(128)} %reduce_sum.9), kind=kLoop, calls=%fused_computation | loop fusion | flops 64 | bytes 516 | tf_op jit(solution)/shard_map/div | solution.py:601
  22.4 0.7 %broadcast_divide_fusion.inverse_ref = f32[64]{0:T(128)S(1)} fusion(f32[64]{0:T(128)S(1)} %copy-done, f32[]{:T(128)} %reduce_sum.9), kind=kLoop, calls=%fused_computation.2 | loop fusion | flops 64 | bytes 516 | tf_op jit(solution)/shard_map/div | solution.py:602
  23.1 18.8 %all-to-all-done.r_ref = f32[16,18,8,128]{3,2,1,0:T(8,128)S(1)} async-done(((f32[16,18,8,128]{3,2,1,0:T(8,128)}), f32[16,18,8,128]{3,2,1,0:T(8,128)S(1)}, u32[]{:S(2)}, u32[]{:S(2)}) %all-to-all-start) | async-done | bytes 1179680 | tf_op jit(solution)/shard_map/all_to_all | solution.py:599
  41.9 7.0 %remap.1 = (f32[64,8,180]{2,1,0:T(8,128)}, f32[64,8,180]{2,1,0:T(8,128)}) custom-call(f32[64]{0:T(128)S(1)} %divide_reduce_fusion.sigma_ref, f32[64]{0:T(128)S(1)} %broadcast_divide_fusion.inverse_ref, f32[1,128]{1,0:T(1,128)S(1)} %pad_bitcast_fusion.row_ref, f32[16,18,8,128]{3,2,1,0:T(8,128)S(1)} %all-to-all-done.r_ref), custom_call_target="tpu_custom_call" | custom-call | tf_op jit(solution)/shard_map/remap/pallas_call | solution.py:605
  (1 shorter events, 0.0 us)
Async XLA Ops:
  2.5 8.4 %collective-permute-start = (f32[3,4,2880]{2,1,0:T(4,128)S(1)}, f32[3,4,2880]{2,1,0:T(4,128)S(1)}, u32[]{:S(2)}, u32[]{:S(2)}) collective-permute-start(f32[3,4,2880]{2,1,0:T(4,128)S(1)} %get-tuple-element.10.last_ref), channel_id=1, source_target_pairs={{0,16},{16,32},{32,48},{48,64},{64,80},{80,96},{96,112},{112,128},... | collective-permute-start | bytes 414728 | tf_op jit(solution)/shard_map/ppermute | solution.py:565
  4.4 7.5 %collective-permute-start.1 = (f32[3,4,2880]{2,1,0:T(4,128)S(1)}, f32[3,4,2880]{2,1,0:T(4,128)S(1)}, u32[]{:S(2)}, u32[]{:S(2)}) collective-permute-start(f32[3,4,2880]{2,1,0:T(4,128)S(1)} %get-tuple-element.11.first_ref), channel_id=1, source_target_pairs={{16,0},{32,16},{48,32},{64,48},{80,64},{96,80},{112,96},{128,112},... | collective-permute-start | bytes 414728 | tf_op jit(solution)/shard_map/ppermute | solution.py:566
  13.8 7.1 %copy-start = (f32[64]{0:T(128)S(1)}, f32[64]{0:T(128)}, u32[]{:S(2)}) copy-start(f32[64]{0:T(128)} %param.12) | copy-start | bytes 772
  13.8 28.1 %all-to-all-start = ((f32[16,18,8,128]{3,2,1,0:T(8,128)}), f32[16,18,8,128]{3,2,1,0:T(8,128)S(1)}, u32[]{:S(2)}, u32[]{:S(2)}) async-start(f32[16,18,8,128]{3,2,1,0:T(8,128)} %pack.1), calls=%async_computation | async-start | bytes 2359296 | tf_op jit(solution)/shard_map/all_to_all | solution.py:599

commit v4 on v3

--- a/solution.py
+++ b/solution.py
@@ -319,8 +319,8 @@
 
 
 EDGE, AU, BU, CU, FU, AT, BT, CT, FT = range(9)
-BLOCK = 8
-WINDOW = 10
+BLOCK = 16
+WINDOW = 11
 UNROLL = 2
 MARGIN = 1e-5
 
@@ -372,7 +372,7 @@
                     fta, ftb = fta + ha * ta, ftb + hb * tb
         return ea, eb, fua, fub, fta, ftb
 
-    sums = lax.fori_loop(0, PEERS // 2, unpack, (zero,) * 6)
+    sums = lax.fori_loop(0, PEERS // 2, unpack, (zero,) * 6, unroll=4)
     surface = sums[:2]
     inverse = tuple(1.0 / s for s in surface)
     for k in range(WINDOW):
@@ -393,7 +393,7 @@
             y_ref[side, n] = rows[0]
         return 0
 
-    lax.fori_loop(0, LEVELS // 8, tally, 0)
+    lax.fori_loop(0, LEVELS // 8, tally, 0, unroll=2)
     counts = []
     for side, reduce, shift in ((0, jnp.max, -MARGIN), (1, jnp.min, MARGIN)):
         ends = [reduce(y_ref[side, n], axis=1, keepdims=True) for n in range(LEVELS // 8)]

time: 49 us -> 47.5 us (0.969)
  Pallas kernels: 12.3 us -> 10.5 us
    pallas_call x1, Pallas kernels: 6.99 us -> 5.21 us  [local(): pl.pallas_call(remap_kernel, name='remap', compiler_params=pltpu.Compiler...]
  transfers between devices with their start and end apart: 3 -> 3, of which waited for: 2 -> 2; matrix products, arithmetic and copies ran while one was open for 4% -> 5% of each run, Pallas kernels for 3% -> 3%
where the time goes in v4:
time: 47.5 us; the launch traced here: 47.1 us
  waiting for transfers between devices  19.8 us (42%)
  starting transfers between devices  13.8 us (29%)
  Pallas kernels  10.5 us (22%)
  other arithmetic  2.1 us (4%)
  between operations  0.73 us (2%)
    all_to_all x1, waiting for transfers between devices, local(): lax.all_to_all(outgoing, 'lev', split_axis=0, concat_axis=0, tiled=True)  18.8 us
    all_to_all x1, starting transfers between devices, local(): lax.all_to_all(outgoing, 'lev', split_axis=0, concat_axis=0, tiled=True)  7.05 us
    pallas_call x1, Pallas kernels, local(): pl.pallas_call(remap_kernel, name='remap', compiler_params=pltpu.Compiler...  5.21 us
    ppermute x1, starting transfers between devices, local(): north = lax.ppermute(first, 'lat', down)  4.85 us
    ppermute x1, starting transfers between devices, local(): south = lax.ppermute(last, 'lat', up)  1.92 us
    pallas_call x1, Pallas kernels, local(): pl.pallas_call(pack_kernel, name='pack', compiler_params=pltpu.CompilerPa...  1.89 us
    pallas_call x1, Pallas kernels, local(): pl.pallas_call(load_kernel, name='load', compiler_params=pltpu.CompilerPa...  1.85 us
    pallas_call x1, Pallas kernels, local(): pl.pallas_call(advance_kernel, name='advance', compiler_params=pltpu.Comp...  1.59 us
  transfers between devices with their start and end apart: 3, of which 2 were waited for; matrix products, arithmetic and copies ran while one was open for 5% of the time, Pallas kernels for 3%

profile of v4, /device:TPU:128, one launch (start us, length us, event | category | flops | bytes accessed | tf_op | source)
XLA Modules:
  0.0 47.1 jit_solution(4446738266938436818)
XLA Ops:
  0.6 1.9 %load.1 = (f32[4,8,2880]{2,1,0:T(8,128)S(1)}, f32[4,8,2880]{2,1,0:T(8,128)S(1)}, f32[4,8,2880]{2,1,0:T(8,128)S(1)}, f32[4,8,2880]{2,1,0:T(8,128)S(1)}, f32[3,4,2...) custom-call(s32[1]{0:T(128)} %bitcast.2.band_ref, f32[4,8,2880]{2,1,0:T(8,128)} %u_hbm.1, f32[4,8,2880]{2,1,0:T(8,128)} %v_hbm.1, ...), custom_call_target="tpu_custom_call" | custom-call | tf_op jit(solution)/shard_map/load/pallas_call | solution.py:545
  2.5 1.9 %collective-permute-start = (f32[3,4,2880]{2,1,0:T(4,128)S(1)}, f32[3,4,2880]{2,1,0:T(4,128)S(1)}, u32[]{:S(2)}, u32[]{:S(2)}) collective-permute-start(f32[3,4,2880]{2,1,0:T(4,128)S(1)} %get-tuple-element.10.last_ref), channel_id=1, source_target_pairs={{0,16},{16,32},{32,48},{48,64},{64,80},{80,96},{96,112},{112,128},... | collective-permute-start | bytes 414728 | tf_op jit(solution)/shard_map/ppermute | solution.py:565
  4.4 4.9 %collective-permute-start.1 = (f32[3,4,2880]{2,1,0:T(4,128)S(1)}, f32[3,4,2880]{2,1,0:T(4,128)S(1)}, u32[]{:S(2)}, u32[]{:S(2)}) collective-permute-start(f32[3,4,2880]{2,1,0:T(4,128)S(1)} %get-tuple-element.11.first_ref), channel_id=1, source_target_pairs={{16,0},{32,16},{48,32},{64,48},{80,64},{96,80},{112,96},{128,112},... | collective-permute-start | bytes 414728 | tf_op jit(solution)/shard_map/ppermute | solution.py:566
  9.3 1.6 %advance.1 = (f32[2,4,8,2944]{3,2,1,0:T(8,128)S(1)}, f32[16,18,8,128]{3,2,1,0:T(8,128)}) custom-call(f32[4,8,2880]{2,1,0:T(8,128)S(1)} %get-tuple-element.12.u_ref, f32[4,8,2880]{2,1,0:T(8,128)S(1)} %get-tuple-element.13.v_ref, f32[4,8,2880]{2,1,0:T(8,128)S(1)} %get-tuple-element.14.h_ref, f32[4,8,2880]{2,1,0:T(8,128)S(1)} %get-tuple-element.15.t_ref), custom_call_target="tpu_custom_call" | custom-call | tf_op jit(solution)/shard_map/advance/pallas_call | solution.py:569
  10.9 0.0 collective-permute-done.south_ref
  10.9 1.0 %collective-permute-done.1.north_ref = f32[3,4,2880]{2,1,0:T(4,128)S(1)} collective-permute-done((f32[3,4,2880]{2,1,0:T(4,128)S(1)}, f32[3,4,2880]{2,1,0:T(4,128)S(1)}, u32[]{:S(2)}, u32[]{:S(2)}) %collective-permute-start.1) | collective-permute-done | bytes 138272 | tf_op jit(solution)/shard_map/ppermute | solution.py:566
  11.9 1.9 %pack.1 = f32[16,18,8,128]{3,2,1,0:T(8,128)} custom-call(f32[3,4,2880]{2,1,0:T(4,128)S(1)} %collective-permute-done.south_ref, f32[3,4,2880]{2,1,0:T(4,128)S(1)} %collective-permute-done.1.north_ref, f32[3,4,2880]{2,1,0:T(4,128)S(1)} %get-tuple-element.11.first_ref, f32[3,4,2880]{2,1,0:T(4,128)S(1)} %get-tuple-element.10.last_ref, ...), custom_call_target="tpu_custom_call", output_to_operand_aliasing={{}: (5, {})} | custom-call | tf_op jit(solution)/shard_map/pack/pallas_call | solution.py:582
  13.8 0.0 copy-start
  13.8 7.0 %all-to-all-start = ((f32[16,18,8,128]{3,2,1,0:T(8,128)}), f32[16,18,8,128]{3,2,1,0:T(8,128)S(1)}, u32[]{:S(2)}, u32[]{:S(2)}) async-start(f32[16,18,8,128]{3,2,1,0:T(8,128)} %pack.1), calls=%async_computation | async-start | bytes 2359296 | tf_op jit(solution)/shard_map/all_to_all | solution.py:599
  20.8 0.0 copy-done
  20.8 0.6 %reduce_sum.9 = f32[]{:T(128)} reduce(f32[64]{0:T(128)S(1)} %copy-done, f32[]{:T(128)} %constant.5.clone.1), dimensions={0}, to_apply=%region_1.0 | reduce | flops 63 | bytes 264 | tf_op jit(solution)/shard_map/reduce_sum | solution.py:600
  21.5 0.1 copy.11
  21.5 0.1 reduce-window.9
  21.6 0.8 %divide_reduce_fusion.sigma_ref = f32[64]{0:T(128)S(1)} fusion(f32[64,1]{1,0:T(8,128)S(1)} %reduce-window.9, f32[]{:T(128)} %reduce_sum.9), kind=kLoop, calls=%fused_computation | loop fusion | flops 64 | bytes 516 | tf_op jit(solution)/shard_map/div | solution.py:601
  22.4 0.7 %broadcast_divide_fusion.inverse_ref = f32[64]{0:T(128)S(1)} fusion(f32[64]{0:T(128)S(1)} %copy-done, f32[]{:T(128)} %reduce_sum.9), kind=kLoop, calls=%fused_computation.2 | loop fusion | flops 64 | bytes 516 | tf_op jit(solution)/shard_map/div | solution.py:602
  23.1 18.8 %all-to-all-done.r_ref = f32[16,18,8,128]{3,2,1,0:T(8,128)S(1)} async-done(((f32[16,18,8,128]{3,2,1,0:T(8,128)}), f32[16,18,8,128]{3,2,1,0:T(8,128)S(1)}, u32[]{:S(2)}, u32[]{:S(2)}) %all-to-all-start) | async-done | bytes 1179680 | tf_op jit(solution)/shard_map/all_to_all | solution.py:599
  41.9 5.2 %remap.1 = (f32[64,8,180]{2,1,0:T(8,128)}, f32[64,8,180]{2,1,0:T(8,128)}) custom-call(f32[64]{0:T(128)S(1)} %divide_reduce_fusion.sigma_ref, f32[64]{0:T(128)S(1)} %broadcast_divide_fusion.inverse_ref, f32[1,128]{1,0:T(1,128)S(1)} %pad_bitcast_fusion.row_ref, f32[16,18,8,128]{3,2,1,0:T(8,128)S(1)} %all-to-all-done.r_ref), custom_call_target="tpu_custom_call" | custom-call | tf_op jit(solution)/shard_map/remap/pallas_call | solution.py:605
  (1 shorter events, 0.0 us)
Async XLA Ops:
  2.5 8.4 %collective-permute-start = (f32[3,4,2880]{2,1,0:T(4,128)S(1)}, f32[3,4,2880]{2,1,0:T(4,128)S(1)}, u32[]{:S(2)}, u32[]{:S(2)}) collective-permute-start(f32[3,4,2880]{2,1,0:T(4,128)S(1)} %get-tuple-element.10.last_ref), channel_id=1, source_target_pairs={{0,16},{16,32},{32,48},{48,64},{64,80},{80,96},{96,112},{112,128},... | collective-permute-start | bytes 414728 | tf_op jit(solution)/shard_map/ppermute | solution.py:565
  4.4 7.5 %collective-permute-start.1 = (f32[3,4,2880]{2,1,0:T(4,128)S(1)}, f32[3,4,2880]{2,1,0:T(4,128)S(1)}, u32[]{:S(2)}, u32[]{:S(2)}) collective-permute-start(f32[3,4,2880]{2,1,0:T(4,128)S(1)} %get-tuple-element.11.first_ref), channel_id=1, source_target_pairs={{16,0},{32,16},{48,32},{64,48},{80,64},{96,80},{112,96},{128,112},... | collective-permute-start | bytes 414728 | tf_op jit(solution)/shard_map/ppermute | solution.py:566
  13.8 7.1 %copy-start = (f32[64]{0:T(128)S(1)}, f32[64]{0:T(128)}, u32[]{:S(2)}) copy-start(f32[64]{0:T(128)} %param.12) | copy-start | bytes 772
  13.8 28.1 %all-to-all-start = ((f32[16,18,8,128]{3,2,1,0:T(8,128)}), f32[16,18,8,128]{3,2,1,0:T(8,128)S(1)}, u32[]{:S(2)}, u32[]{:S(2)}) async-start(f32[16,18,8,128]{3,2,1,0:T(8,128)} %pack.1), calls=%async_computation | async-start | bytes 2359296 | tf_op jit(solution)/shard_map/all_to_all | solution.py:599

commit v5 on v4

--- a/solution.py
+++ b/solution.py
@@ -300,7 +300,7 @@
             n_ref[1, l, :, at] = new_h
         return 0
 
-    lax.fori_loop(0, LEV_DEV, finish, 0)
+    lax.fori_loop(0, LEV_DEV, finish, 0, unroll=2)
 
     def put(pair, f):
         def fetch(l, i):

time: 47.5 us -> 47.3 us (level)
  no operation moved by 1% of the time
where the time goes in v5:
time: 47.3 us; the launch traced here: 47.1 us
  waiting for transfers between devices  19.8 us (42%)
  starting transfers between devices  13.8 us (29%)
  Pallas kernels  10.5 us (22%)
  other arithmetic  2.1 us (4%)
  between operations  0.73 us (2%)
    all_to_all x1, waiting for transfers between devices, local(): lax.all_to_all(outgoing, 'lev', split_axis=0, concat_axis=0, tiled=True)  18.8 us
    all_to_all x1, starting transfers between devices, local(): lax.all_to_all(outgoing, 'lev', split_axis=0, concat_axis=0, tiled=True)  7.05 us
    pallas_call x1, Pallas kernels, local(): pl.pallas_call(remap_kernel, name='remap', compiler_params=pltpu.Compiler...  5.21 us
    ppermute x1, starting transfers between devices, local(): north = lax.ppermute(first, 'lat', down)  4.85 us
    ppermute x1, starting transfers between devices, local(): south = lax.ppermute(last, 'lat', up)  1.92 us
    pallas_call x1, Pallas kernels, local(): pl.pallas_call(pack_kernel, name='pack', compiler_params=pltpu.CompilerPa...  1.87 us
    pallas_call x1, Pallas kernels, local(): pl.pallas_call(load_kernel, name='load', compiler_params=pltpu.CompilerPa...  1.85 us
    pallas_call x1, Pallas kernels, local(): pl.pallas_call(advance_kernel, name='advance', compiler_params=pltpu.Comp...  1.59 us
  transfers between devices with their start and end apart: 3, of which 2 were waited for; matrix products, arithmetic and copies ran while one was open for 5% of the time, Pallas kernels for 3%

profile of v5, /device:TPU:128, one launch (start us, length us, event | category | flops | bytes accessed | tf_op | source)
XLA Modules:
  0.0 47.1 jit_solution(1414315253839064396)
XLA Ops:
  0.6 1.9 %load.1 = (f32[4,8,2880]{2,1,0:T(8,128)S(1)}, f32[4,8,2880]{2,1,0:T(8,128)S(1)}, f32[4,8,2880]{2,1,0:T(8,128)S(1)}, f32[4,8,2880]{2,1,0:T(8,128)S(1)}, f32[3,4,2...) custom-call(s32[1]{0:T(128)} %bitcast.2.band_ref, f32[4,8,2880]{2,1,0:T(8,128)} %u_hbm.1, f32[4,8,2880]{2,1,0:T(8,128)} %v_hbm.1, ...), custom_call_target="tpu_custom_call" | custom-call | tf_op jit(solution)/shard_map/load/pallas_call | solution.py:545
  2.5 1.9 %collective-permute-start = (f32[3,4,2880]{2,1,0:T(4,128)S(1)}, f32[3,4,2880]{2,1,0:T(4,128)S(1)}, u32[]{:S(2)}, u32[]{:S(2)}) collective-permute-start(f32[3,4,2880]{2,1,0:T(4,128)S(1)} %get-tuple-element.10.last_ref), channel_id=1, source_target_pairs={{0,16},{16,32},{32,48},{48,64},{64,80},{80,96},{96,112},{112,128},... | collective-permute-start | bytes 414728 | tf_op jit(solution)/shard_map/ppermute | solution.py:565
  4.4 4.9 %collective-permute-start.1 = (f32[3,4,2880]{2,1,0:T(4,128)S(1)}, f32[3,4,2880]{2,1,0:T(4,128)S(1)}, u32[]{:S(2)}, u32[]{:S(2)}) collective-permute-start(f32[3,4,2880]{2,1,0:T(4,128)S(1)} %get-tuple-element.11.first_ref), channel_id=1, source_target_pairs={{16,0},{32,16},{48,32},{64,48},{80,64},{96,80},{112,96},{128,112},... | collective-permute-start | bytes 414728 | tf_op jit(solution)/shard_map/ppermute | solution.py:566
  9.3 1.6 %advance.1 = (f32[2,4,8,2944]{3,2,1,0:T(8,128)S(1)}, f32[16,18,8,128]{3,2,1,0:T(8,128)}) custom-call(f32[4,8,2880]{2,1,0:T(8,128)S(1)} %get-tuple-element.12.u_ref, f32[4,8,2880]{2,1,0:T(8,128)S(1)} %get-tuple-element.13.v_ref, f32[4,8,2880]{2,1,0:T(8,128)S(1)} %get-tuple-element.14.h_ref, f32[4,8,2880]{2,1,0:T(8,128)S(1)} %get-tuple-element.15.t_ref), custom_call_target="tpu_custom_call" | custom-call | tf_op jit(solution)/shard_map/advance/pallas_call | solution.py:569
  10.9 0.0 collective-permute-done.south_ref
  10.9 1.0 %collective-permute-done.1.north_ref = f32[3,4,2880]{2,1,0:T(4,128)S(1)} collective-permute-done((f32[3,4,2880]{2,1,0:T(4,128)S(1)}, f32[3,4,2880]{2,1,0:T(4,128)S(1)}, u32[]{:S(2)}, u32[]{:S(2)}) %collective-permute-start.1) | collective-permute-done | bytes 138272 | tf_op jit(solution)/shard_map/ppermute | solution.py:566
  11.9 1.9 %pack.1 = f32[16,18,8,128]{3,2,1,0:T(8,128)} custom-call(f32[3,4,2880]{2,1,0:T(4,128)S(1)} %collective-permute-done.south_ref, f32[3,4,2880]{2,1,0:T(4,128)S(1)} %collective-permute-done.1.north_ref, f32[3,4,2880]{2,1,0:T(4,128)S(1)} %get-tuple-element.11.first_ref, f32[3,4,2880]{2,1,0:T(4,128)S(1)} %get-tuple-element.10.last_ref, ...), custom_call_target="tpu_custom_call", output_to_operand_aliasing={{}: (5, {})} | custom-call | tf_op jit(solution)/shard_map/pack/pallas_call | solution.py:582
  13.8 0.0 copy-start
  13.8 7.0 %all-to-all-start = ((f32[16,18,8,128]{3,2,1,0:T(8,128)}), f32[16,18,8,128]{3,2,1,0:T(8,128)S(1)}, u32[]{:S(2)}, u32[]{:S(2)}) async-start(f32[16,18,8,128]{3,2,1,0:T(8,128)} %pack.1), calls=%async_computation | async-start | bytes 2359296 | tf_op jit(solution)/shard_map/all_to_all | solution.py:599
  20.8 0.0 copy-done
  20.8 0.6 %reduce_sum.9 = f32[]{:T(128)} reduce(f32[64]{0:T(128)S(1)} %copy-done, f32[]{:T(128)} %constant.5.clone.1), dimensions={0}, to_apply=%region_1.0 | reduce | flops 63 | bytes 264 | tf_op jit(solution)/shard_map/reduce_sum | solution.py:600
  21.4 0.1 copy.11
  21.5 0.1 reduce-window.9
  21.6 0.8 %divide_reduce_fusion.sigma_ref = f32[64]{0:T(128)S(1)} fusion(f32[64,1]{1,0:T(8,128)S(1)} %reduce-window.9, f32[]{:T(128)} %reduce_sum.9), kind=kLoop, calls=%fused_computation | loop fusion | flops 64 | bytes 516 | tf_op jit(solution)/shard_map/div | solution.py:601
  22.4 0.7 %broadcast_divide_fusion.inverse_ref = f32[64]{0:T(128)S(1)} fusion(f32[64]{0:T(128)S(1)} %copy-done, f32[]{:T(128)} %reduce_sum.9), kind=kLoop, calls=%fused_computation.2 | loop fusion | flops 64 | bytes 516 | tf_op jit(solution)/shard_map/div | solution.py:602
  23.1 18.8 %all-to-all-done.r_ref = f32[16,18,8,128]{3,2,1,0:T(8,128)S(1)} async-done(((f32[16,18,8,128]{3,2,1,0:T(8,128)}), f32[16,18,8,128]{3,2,1,0:T(8,128)S(1)}, u32[]{:S(2)}, u32[]{:S(2)}) %all-to-all-start) | async-done | bytes 1179680 | tf_op jit(solution)/shard_map/all_to_all | solution.py:599
  41.9 5.2 %remap.1 = (f32[64,8,180]{2,1,0:T(8,128)}, f32[64,8,180]{2,1,0:T(8,128)}) custom-call(f32[64]{0:T(128)S(1)} %divide_reduce_fusion.sigma_ref, f32[64]{0:T(128)S(1)} %broadcast_divide_fusion.inverse_ref, f32[1,128]{1,0:T(1,128)S(1)} %pad_bitcast_fusion.row_ref, f32[16,18,8,128]{3,2,1,0:T(8,128)S(1)} %all-to-all-done.r_ref), custom_call_target="tpu_custom_call" | custom-call | tf_op jit(solution)/shard_map/remap/pallas_call | solution.py:605
  (1 shorter events, 0.0 us)
Async XLA Ops:
  2.5 8.4 %collective-permute-start = (f32[3,4,2880]{2,1,0:T(4,128)S(1)}, f32[3,4,2880]{2,1,0:T(4,128)S(1)}, u32[]{:S(2)}, u32[]{:S(2)}) collective-permute-start(f32[3,4,2880]{2,1,0:T(4,128)S(1)} %get-tuple-element.10.last_ref), channel_id=1, source_target_pairs={{0,16},{16,32},{32,48},{48,64},{64,80},{80,96},{96,112},{112,128},... | collective-permute-start | bytes 414728 | tf_op jit(solution)/shard_map/ppermute | solution.py:565
  4.4 7.5 %collective-permute-start.1 = (f32[3,4,2880]{2,1,0:T(4,128)S(1)}, f32[3,4,2880]{2,1,0:T(4,128)S(1)}, u32[]{:S(2)}, u32[]{:S(2)}) collective-permute-start(f32[3,4,2880]{2,1,0:T(4,128)S(1)} %get-tuple-element.11.first_ref), channel_id=1, source_target_pairs={{16,0},{32,16},{48,32},{64,48},{80,64},{96,80},{112,96},{128,112},... | collective-permute-start | bytes 414728 | tf_op jit(solution)/shard_map/ppermute | solution.py:566
  13.8 7.1 %copy-start = (f32[64]{0:T(128)S(1)}, f32[64]{0:T(128)}, u32[]{:S(2)}) copy-start(f32[64]{0:T(128)} %param.12) | copy-start | bytes 772
  13.8 28.1 %all-to-all-start = ((f32[16,18,8,128]{3,2,1,0:T(8,128)}), f32[16,18,8,128]{3,2,1,0:T(8,128)S(1)}, u32[]{:S(2)}, u32[]{:S(2)}) async-start(f32[16,18,8,128]{3,2,1,0:T(8,128)} %pack.1), calls=%async_computation | async-start | bytes 2359296 | tf_op jit(solution)/shard_map/all_to_all | solution.py:599
